TPU v7x, 512 devices: a whole 4x8x8 slice. The times are simulated.
512 devices in a mesh: view: 16 (over y, core), row: 4 (over x), col: 8 (over z).
Axes of the slice: x: 4, y: 8, z: 8, core: 2. Of those that a mesh axis runs over, the one named last changes fastest.
Arguments:
- volume: bfloat16 [256, 1024, 1024], P('view', 'row', 'col'), may hold values from -5 to 5
- tf_color: float32 [3, 16], replicated, may hold values from 0 to 1
- tf_opacity: float32 [16], replicated, may hold values from 0.2 to 4
Outputs:
- picture: float32 [4, 16, 64, 1024], P(None, 'view', 'row', 'col')
All inputs are finite; a program needn't handle non-finite values.
Results may differ from a plain program's by a relative error of at most 0.00095.
Values may be sent and summed in bfloat16 or wider, within the bound.
A program may use at most 64 MiB of HBM per device.

v0:
```python
import jax
import jax.numpy as jnp
from jax import lax
from jax.sharding import PartitionSpec as P

LIGHT_Z = 0.48
LIGHT_Y = 0.6
LIGHT_X = 0.64
VALUE_LOW = -3.0
VALUE_HIGH = 3.0


def extended(cells, sides, width):
    for axis, dim in sides:
        count = lax.axis_size(axis)
        ends = count - 1
        head = lax.slice_in_dim(cells, 0, width, axis=dim)
        tail = lax.slice_in_dim(cells, cells.shape[dim] - width, cells.shape[dim], axis=dim)
        cells = jnp.concatenate(
            [
                lax.ppermute(tail, axis, [(i, (i + 1) % count) for i in range(ends)]),
                cells,
                lax.ppermute(head, axis, [((i + 1) % count, i) for i in range(ends)]),
            ],
            axis=dim,
        )
    return cells


def classify(three_slices, tf_color, tf_opacity, depth_total):
    centre = three_slices[1, 1:-1, 1:-1]
    grad_z = (three_slices[2, 1:-1, 1:-1] - three_slices[0, 1:-1, 1:-1]) * 0.5
    grad_y = (three_slices[1, 2:, 1:-1] - three_slices[1, :-2, 1:-1]) * 0.5
    grad_x = (three_slices[1, 1:-1, 2:] - three_slices[1, 1:-1, :-2]) * 0.5
    grad_sq = grad_z * grad_z + grad_y * grad_y + grad_x * grad_x
    shading = 0.35 + 0.65 * jnp.abs(
        LIGHT_Z * grad_z + LIGHT_Y * grad_y + LIGHT_X * grad_x
    ) / jnp.sqrt(grad_sq + 1.0)
    knot_count = tf_color.shape[1]
    scaled = jnp.clip(
        (centre - VALUE_LOW) * ((knot_count - 1) / (VALUE_HIGH - VALUE_LOW)), 0.0, knot_count - 1.0
    )
    places = jnp.arange(knot_count, dtype=jnp.float32).reshape(knot_count, 1)
    weights = jnp.maximum(0.0, 1.0 - jnp.abs(scaled.reshape(1, -1) - places))
    colour = jnp.dot(tf_color, weights, precision=lax.Precision.HIGHEST).reshape(
        (3,) + centre.shape
    )
    extinction = jnp.dot(
        tf_opacity.reshape(1, knot_count), weights, precision=lax.Precision.HIGHEST
    ).reshape(centre.shape)
    opacity_cell = 1.0 - jnp.exp(
        -2.0 * extinction * (0.2 + grad_sq / (grad_sq + 1.0)) / depth_total
    )
    return (colour * shading * opacity_cell, opacity_cell)


def composite_over(nearer, farther):
    return nearer + (1.0 - nearer[3:4]) * farther


def on_device(volume, tf_color, tf_opacity):
    view_count = lax.axis_size("view")
    slice_count, height, tile_width = volume.shape
    depth_total = slice_count * view_count
    padded = extended(volume, (("view", 0), ("row", 1), ("col", 2)), 1)

    def advance(slice_index, running):
        colour_sum, through = running
        three_slices = lax.dynamic_slice_in_dim(padded, slice_index, 3, 0).astype(jnp.float32)
        emission, opacity_cell = classify(three_slices, tf_color, tf_opacity, depth_total)
        return (colour_sum + through * emission, through * (1.0 - opacity_cell))

    initial = (
        jnp.zeros((3, height, tile_width), jnp.float32),
        jnp.ones((height, tile_width), jnp.float32),
    )
    colour_sum, through = lax.fori_loop(0, slice_count, advance, initial)
    partial_image = jnp.concatenate([colour_sum, (1.0 - through)[None]], axis=0)
    tile_rows = height // view_count
    row_blocks = partial_image.reshape(4, view_count, tile_rows, tile_width)
    received = lax.all_to_all(
        row_blocks.astype(jnp.bfloat16), "view", split_axis=1, concat_axis=1, tiled=True
    ).astype(row_blocks.dtype)

    def fold_layer(layer_index, running):
        one_layer = lax.dynamic_index_in_dim(received, layer_index, 1, keepdims=False)
        return composite_over(running, one_layer)

    initial_image = jnp.zeros((4,) + received.shape[2:], jnp.float32)
    final = lax.fori_loop(0, received.shape[1], fold_layer, initial_image)
    return final.reshape(4, 1, tile_rows, tile_width)


def solution(mesh):
    placed = (P("view", "row", "col"), P(), P())
    return jax.shard_map(
        on_device,
        mesh=mesh,
        in_specs=placed,
        out_specs=P(None, "view", "row", "col"),
        check_vma=False,
    )
```

profile of v0, /device:TPU:1, one launch (start us, length us, event | category | flops | bytes accessed | tf_op | source)
XLA Modules:
  0.0 148.9 jit_solution(3363448268074951401)
XLA Ops:
  0.0 1.9 %copy.19 = bf16[16,256,128]{2,0,1:T(8,128)(2,1)S(1)} copy(bf16[16,256,128]{2,1,0:T(8,128)(2,1)} %param.7) | data formatting | bytes 2097152 | tf_op args[0]
  2.1 4.6 %collective-permute-start = (bf16[1,256,128]{2,0,1:T(2,128)(2,1)S(1)}, bf16[1,256,128]{2,0,1:T(2,128)(2,1)S(1)}, u32[]{:S(2)}, u32[]{:S(2)}) collective-permute-start(bf16[1,256,128]{2,0,1:T(2,128)(2,1)S(1)} %get-tuple-element.312), channel_id=1, source_target_pairs={{0,32},{32,64},{64,96},{96,128},{128,160},{160,192},{192,224},{224... | collective-permute-start | bytes 196616 | tf_op jit(solution)/shard_map/ppermute | solution.py:21
  6.7 5.5 %collective-permute-start.1 = (bf16[1,256,128]{2,0,1:T(2,128)(2,1)S(1)}, bf16[1,256,128]{2,0,1:T(2,128)(2,1)S(1)}, u32[]{:S(2)}, u32[]{:S(2)}) collective-permute-start(bf16[1,256,128]{2,0,1:T(2,128)(2,1)S(1)} %get-tuple-element.313), channel_id=1, source_target_pairs={{32,0},{64,32},{96,64},{128,96},{160,128},{192,160},{224,192},{256... | collective-permute-start | bytes 196616 | tf_op jit(solution)/shard_map/ppermute | solution.py:23
  13.2 3.0 %collective-permute-start.2 = (bf16[18,1,128]{2,0,1:T(8,128)(2,1)S(1)}, bf16[18,1,128]{2,0,1:T(8,128)(2,1)S(1)}, u32[]{:S(2)}, u32[]{:S(2)}) collective-permute-start(bf16[18,1,128]{2,0,1:T(8,128)(2,1)S(1)} %get-tuple-element.310), channel_id=1, source_target_pairs={{0,8},{8,16},{16,24},{1,9},{9,17},{17,25},{2,10},{10,18},{18,26},{... | collective-permute-start | bytes 13832 | tf_op jit(solution)/shard_map/ppermute | solution.py:21
  17.4 3.1 %collective-permute-done.3 = bf16[18,1,128]{2,0,1:T(8,128)(2,1)S(1)} collective-permute-done((bf16[18,1,128]{2,0,1:T(8,128)(2,1)S(1)}, bf16[18,1,128]{2,0,1:T(8,128)(2,1)S(1)}, u32[]{:S(2)}, u32[]{:S(2)}) %collective-permute-start.3) | collective-permute-done | bytes 4640 | tf_op jit(solution)/shard_map/ppermute | solution.py:23
  21.5 1.9 %fusion.41 = (bf16[18,258,1]{2,0,1:T(8,128)(2,1)}, bf16[18,258,1]{2,0,1:T(8,128)(2,1)S(1)}) fusion(bf16[18,258,128]{2,0,1:T(8,128)(2,1)S(1)} %pad_maximum_fusion.1), kind=kLoop, calls=%fused_computation.59 | loop fusion | bytes 37152 | tf_op jit(solution)/shard_map/slice | solution.py:18
  23.4 3.1 %copy.22 = bf16[18,258,1]{1,0,2:T(8,128)(2,1)S(1)} copy(bf16[18,258,1]{2,0,1:T(8,128)(2,1)} %get-tuple-element.308) | data formatting | bytes 18576 | tf_op jit(solution)/shard_map/slice | solution.py:18
  26.5 4.0 %collective-permute-start.4 = (bf16[18,258,1]{1,0,2:T(8,128)(2,1)S(1)}, bf16[18,258,1]{1,0,2:T(8,128)(2,1)S(1)}, u32[]{:S(2)}, u32[]{:S(2)}) collective-permute-start(bf16[18,258,1]{1,0,2:T(8,128)(2,1)S(1)} %copy.22), channel_id=1, source_target_pairs={{0,1},{1,2},{2,3},{3,4},{4,5},{5,6},{6,7},{8,9},{9,10},{10,11},{11... | collective-permute-start | bytes 27872 | tf_op jit(solution)/shard_map/ppermute | solution.py:21
  30.5 2.2 %copy.23 = bf16[18,258,1]{1,0,2:T(8,128)(2,1)S(1)} copy(bf16[18,258,1]{2,0,1:T(8,128)(2,1)S(1)} %get-tuple-element.309) | data formatting | bytes 18576 | tf_op jit(solution)/shard_map/slice | solution.py:17
  32.7 1.5 collective-permute-start.5
  34.3 2.6 %copy.24 = bf16[18,258,1]{2,0,1:T(8,128)(2,1)S(1)} copy(bf16[18,258,1]{1,0,2:T(8,128)(2,1)S(1)} %collective-permute-done.4) | data formatting | bytes 18576 | tf_op jit(solution)/shard_map/ppermute | solution.py:21
  37.9 3.1 %copy.25 = bf16[18,258,1]{2,0,1:T(8,128)(2,1)} copy(bf16[18,258,1]{1,0,2:T(8,128)(2,1)S(1)} %collective-permute-done.5) | data formatting | bytes 18576 | tf_op jit(solution)/shard_map/ppermute | solution.py:23
  41.0 6.2 %pad_maximum_fusion = bf16[18,258,130]{2,0,1:T(8,128)(2,1)S(1)} fusion(bf16[18,258,1]{2,0,1:T(8,128)(2,1)} %copy.25, bf16[18,1,128]{2,0,1:T(8,128)(2,1)S(1)} %collective-permute-done.3, bf16[1,256,128]{2,0,1:T(2,128)(2,1)S(1)} %collective-permute-done.1, bf16[16,256,128]{2,0,1:T(8,128)(2,1)S(1)} %copy.19, bf16[1,256,128]{2,0,1:T(2,128)(2,1)S(1)} %collective-permute-done, ...), kind=kLoop, calls=%fused_computation.52 | loop fusion | flops 8452080 | bytes 2414880 | tf_op jit(solution)/shard_map/concatenate | solution.py:19
  47.2 1.9 %copy.26 = bf16[18,258,130]{2,1,0:T(8,128)(2,1)} copy(bf16[18,258,130]{2,0,1:T(8,128)(2,1)S(1)} %pad_maximum_fusion) | data formatting | bytes 2414880
  49.2 76.1 %while.32 = (s32[]{:T(128)}, f32[3,256,128]{2,1,0:T(8,128)S(1)}, f32[256,128]{1,0:T(8,128)S(1)}, bf16[18,258,130]{2,1,0:T(8,128)(2,1)}, f32[3,16]{1,0:T(4,128)S(1)}, /*index=5*/f32[16]{0:T(128)S(1)}, s32[]{:T(128)}, s32[]{:T(128)}) while((s32[]{:T(128)}, f32[3,256,128]{2,1,0:T(8,128)S(1)}, f32[256,128]{1,0:T(8,128)S(1)}, ...), condition=%wide.region_1.2_spmd.clone, body=%wide.region_0.1_spmd.clone.sunk | while | flops 31426828 | bytes 5715884 | solution.py:77
  50.5 1.5 fusion.58
  55.3 1.5 fusion.58
  57.0 1.5 fusion.57
  60.0 1.5 fusion.58
  61.8 1.5 fusion.57
  66.5 1.5 fusion.57
  74.3 1.5 fusion.58
  76.0 1.5 fusion.57
  79.0 1.5 fusion.58
  80.8 1.5 fusion.57
  83.8 1.5 fusion.58
  85.5 1.5 fusion.57
  88.6 1.5 fusion.58
  90.3 1.5 fusion.57
  95.1 1.5 fusion.57
  126.0 9.6 %all-to-all-start = ((bf16[4,16,16,128]{3,2,0,1:T(8,128)(2,1)}), bf16[4,16,16,128]{3,2,0,1:T(8,128)(2,1)S(1)}, u32[]{:S(2)}, u32[]{:S(2)}) async-start(bf16[4,16,16,128]{3,2,0,1:T(8,128)(2,1)} %copy.27), calls=%async_computation | async-start | bytes 524288 | tf_op jit(solution)/shard_map/all_to_all | solution.py:81
  135.6 11.6 %all-to-all-done = bf16[4,16,16,128]{3,2,0,1:T(8,128)(2,1)S(1)} async-done(((bf16[4,16,16,128]{3,2,0,1:T(8,128)(2,1)}), bf16[4,16,16,128]{3,2,0,1:T(8,128)(2,1)S(1)}, u32[]{:S(2)}, u32[]{:S(2)}) %all-to-all-start) | async-done | bytes 262176 | tf_op jit(solution)/shard_map/all_to_all | solution.py:81
  (153 shorter events, 60.7 us)
Async XLA Ops:
  2.1 10.1 %collective-permute-start = (bf16[1,256,128]{2,0,1:T(2,128)(2,1)S(1)}, bf16[1,256,128]{2,0,1:T(2,128)(2,1)S(1)}, u32[]{:S(2)}, u32[]{:S(2)}) collective-permute-start(bf16[1,256,128]{2,0,1:T(2,128)(2,1)S(1)} %get-tuple-element.312), channel_id=1, source_target_pairs={{0,32},{32,64},{64,96},{96,128},{128,160},{160,192},{192,224},{224... | collective-permute-start | bytes 196616 | tf_op jit(solution)/shard_map/ppermute | solution.py:21
  6.7 6.4 %collective-permute-start.1 = (bf16[1,256,128]{2,0,1:T(2,128)(2,1)S(1)}, bf16[1,256,128]{2,0,1:T(2,128)(2,1)S(1)}, u32[]{:S(2)}, u32[]{:S(2)}) collective-permute-start(bf16[1,256,128]{2,0,1:T(2,128)(2,1)S(1)} %get-tuple-element.313), channel_id=1, source_target_pairs={{32,0},{64,32},{96,64},{128,96},{160,128},{192,160},{224,192},{256... | collective-permute-start | bytes 196616 | tf_op jit(solution)/shard_map/ppermute | solution.py:23
  13.2 4.3 %collective-permute-start.2 = (bf16[18,1,128]{2,0,1:T(8,128)(2,1)S(1)}, bf16[18,1,128]{2,0,1:T(8,128)(2,1)S(1)}, u32[]{:S(2)}, u32[]{:S(2)}) collective-permute-start(bf16[18,1,128]{2,0,1:T(8,128)(2,1)S(1)} %get-tuple-element.310), channel_id=1, source_target_pairs={{0,8},{8,16},{16,24},{1,9},{9,17},{17,25},{2,10},{10,18},{18,26},{... | collective-permute-start | bytes 13832 | tf_op jit(solution)/shard_map/ppermute | solution.py:21
  16.1 4.4 %collective-permute-start.3 = (bf16[18,1,128]{2,0,1:T(8,128)(2,1)S(1)}, bf16[18,1,128]{2,0,1:T(8,128)(2,1)S(1)}, u32[]{:S(2)}, u32[]{:S(2)}) collective-permute-start(bf16[18,1,128]{2,0,1:T(8,128)(2,1)S(1)} %get-tuple-element.311), channel_id=1, source_target_pairs={{8,0},{16,8},{24,16},{9,1},{17,9},{25,17},{10,2},{18,10},{26,18},{... | collective-permute-start | bytes 13832 | tf_op jit(solution)/shard_map/ppermute | solution.py:23
  26.5 7.7 %collective-permute-start.4 = (bf16[18,258,1]{1,0,2:T(8,128)(2,1)S(1)}, bf16[18,258,1]{1,0,2:T(8,128)(2,1)S(1)}, u32[]{:S(2)}, u32[]{:S(2)}) collective-permute-start(bf16[18,258,1]{1,0,2:T(8,128)(2,1)S(1)} %copy.22), channel_id=1, source_target_pairs={{0,1},{1,2},{2,3},{3,4},{4,5},{5,6},{6,7},{8,9},{9,10},{10,11},{11... | collective-permute-start | bytes 27872 | tf_op jit(solution)/shard_map/ppermute | solution.py:21
  32.7 5.1 %collective-permute-start.5 = (bf16[18,258,1]{1,0,2:T(8,128)(2,1)S(1)}, bf16[18,258,1]{1,0,2:T(8,128)(2,1)S(1)}, u32[]{:S(2)}, u32[]{:S(2)}) collective-permute-start(bf16[18,258,1]{1,0,2:T(8,128)(2,1)S(1)} %copy.23), channel_id=1, source_target_pairs={{1,0},{2,1},{3,2},{4,3},{5,4},{6,5},{7,6},{9,8},{10,9},{11,10},{12... | collective-permute-start | bytes 27872 | tf_op jit(solution)/shard_map/ppermute | solution.py:23
  47.2 2.0 %copy-start.1 = (f32[3,16]{1,0:T(4,128)S(1)}, f32[3,16]{1,0:T(4,128)}, u32[]{:S(2)}) copy-start(f32[3,16]{1,0:T(4,128)} %param.8) | copy-start | bytes 580
  47.2 2.0 %copy-start.2 = (f32[16]{0:T(128)S(1)}, f32[16]{0:T(128)}, u32[]{:S(2)}) copy-start(f32[16]{0:T(128)} %param.9) | copy-start | bytes 196
  126.0 21.2 %all-to-all-start = ((bf16[4,16,16,128]{3,2,0,1:T(8,128)(2,1)}), bf16[4,16,16,128]{3,2,0,1:T(8,128)(2,1)S(1)}, u32[]{:S(2)}, u32[]{:S(2)}) async-start(bf16[4,16,16,128]{3,2,0,1:T(8,128)(2,1)} %copy.27), calls=%async_computation | async-start | bytes 524288 | tf_op jit(solution)/shard_map/all_to_all | solution.py:81
  148.3 0.6 copy-start
where the time goes:
time: 151 us; the launch traced here: 149 us
  matrix products  46.6 us (31%)
  other arithmetic  36.2 us (24%)
  starting transfers between devices  29.4 us (19%)
  local copies, waits for them, and re-layouts  18.3 us (12%)
  waiting for transfers between devices  16.6 us (11%)
  loops' own time  1.57 us (1%)
    dot_general x16, matrix products, classify(): jnp.dot(tf_opacity.reshape(1, knot_count), weights, precision=lax.Precisi...  23.3 us
    dot_general x16, matrix products, classify(): jnp.dot(tf_color, weights, precision=lax.Precision.HIGHEST)  23.3 us
    convert_element_type x16, other arithmetic, advance(): lax.dynamic_slice_in_dim(padded, slice_index, 3, 0).astype(jnp.float32)  16.9 us
    all_to_all x1, waiting for transfers between devices, on_device(): lax.all_to_all(row_blocks.astype(jnp.bfloat16), 'view', split_axis=1, con...  11.6 us
    ppermute x3, starting transfers between devices, extended(): lax.ppermute(tail, axis, [(i, (i + 1) % count) for i in range(ends)])  11.5 us
    all_to_all x1, starting transfers between devices, on_device(): lax.all_to_all(row_blocks.astype(jnp.bfloat16), 'view', split_axis=1, con...  9.59 us
    ppermute x3, starting transfers between devices, extended(): lax.ppermute(head, axis, [((i + 1) % count, i) for i in range(ends)])  8.23 us
    concatenate x2, other arithmetic, extended(): jnp.concatenate([lax.ppermute(tail, axis, [(i, (i + 1) % count) for i in...  7.19 us
  transfers between devices with their start and end apart: 7, of which 4 were waited for; matrix products, arithmetic and copies ran while one was open for 3% of the time, Pallas kernels for 0%

commit v1 on v0

v1 whole, which is shorter than its diff:
```python
import math

import jax
import jax.numpy as jnp
from jax import lax
from jax.experimental import pallas as pl
from jax.experimental.pallas import tpu as pltpu
from jax.sharding import PartitionSpec as P

LIGHT_Z = 0.48
LIGHT_Y = 0.6
LIGHT_X = 0.64
VALUE_LOW = -3.0
VALUE_HIGH = 3.0
AMBIENT = 0.35
DIFFUSE = 0.65

MESH = pl.DeviceIdType.MESH
LANES = 128
STRIP = 16
HALF = 8


def tables_of(color_ref, opacity_ref, knots, opacity_scale):
    lane = lax.broadcasted_iota(jnp.int32, (HALF, LANES), 1)
    place = lane.astype(jnp.float32)
    pairs = []
    for channel in range(4):
        values = jnp.zeros((HALF, LANES), jnp.float32)
        for k in range(knots):
            entry = color_ref[channel, k] if channel < 3 else opacity_ref[k] * opacity_scale
            values = jnp.where(lane == k, entry, values)
        slope = pltpu.roll(values, LANES - 1, 1) - values
        slope = jnp.where(lane < knots - 1, slope, 0.0)
        pairs.append((values - place * slope, slope))
    return pairs


def look_up(table, index):
    return jnp.take_along_axis(table, index, axis=1, mode="promise_in_bounds")


def kernel(
    counts,
    volume,
    color_ref,
    opacity_ref,
    out_ref,
    cells,
    edges,
    edges_left,
    edges_right,
    across,
    picked,
    outgoing,
    arrived,
    load_sem,
    halo_send,
    halo_recv,
    part_send,
    part_recv,
):
    views, rows, cols = counts
    depth, height, _ = volume.shape
    knots = color_ref.shape[1]
    v, r, c = lax.axis_index("view"), lax.axis_index("row"), lax.axis_index("col")
    body = pl.ds(STRIP, height)

    load = pltpu.make_async_copy(volume, cells.at[pl.ds(1, depth), body], load_sem)
    load.start()

    barrier = pltpu.get_barrier_semaphore()
    for step in range(1, views):
        pl.semaphore_signal(barrier, inc=1, device_id={"view": lax.rem(v + step, views)}, device_id_type=MESH)
    beside = [
        (v > 0, {"view": v - 1}),
        (v < views - 1, {"view": v + 1}),
        (r > 0, {"row": r - 1}),
        (r < rows - 1, {"row": r + 1}),
        (c > 0, {"col": c - 1}),
        (c < cols - 1, {"col": c + 1}),
    ]
    for there, where in beside[2:]:

        @pl.when(there)
        def _():
            pl.semaphore_signal(barrier, inc=1, device_id=where, device_id_type=MESH)

    expected = views - 1
    for there, _ in beside[2:]:
        expected = expected + there.astype(jnp.int32)
    pl.semaphore_wait(barrier, expected)

    sources = [
        volume.at[pl.ds(0, 1)],
        volume.at[pl.ds(depth - 1, 1)],
        volume.at[:, pl.ds(0, STRIP)],
        volume.at[:, pl.ds(height - STRIP, STRIP)],
        edges,
        edges,
    ]
    landings = [
        cells.at[pl.ds(depth + 1, 1), body],
        cells.at[pl.ds(0, 1), body],
        cells.at[pl.ds(1, depth), pl.ds(STRIP + height, STRIP)],
        cells.at[pl.ds(1, depth), pl.ds(0, STRIP)],
        edges_right,
        edges_left,
    ]
    copies = [
        pltpu.make_async_remote_copy(
            src_ref=sources[i],
            dst_ref=landings[i],
            send_sem=halo_send.at[i],
            recv_sem=halo_recv.at[i],
            device_id=beside[i][1],
            device_id_type=MESH,
        )
        for i in range(6)
    ]
    for i in range(4):

        @pl.when(beside[i][0])
        def _():
            copies[i].start()

    for i in range(6):

        @pl.when(jnp.logical_not(beside[i ^ 1][0]))
        def _():
            landings[i][...] = jnp.zeros(landings[i].shape, landings[i].dtype)

    tables = tables_of(color_ref, opacity_ref, knots, -8.0 * math.log2(math.e) / (depth * views))

    k = lax.broadcasted_iota(jnp.int32, (2 * LANES, LANES), 0)
    n = lax.broadcasted_iota(jnp.int32, (2 * LANES, LANES), 1)
    beyond = k - LANES
    plus = ((k < LANES) & (k == n + 1)) | ((beyond >= depth) & (beyond < 2 * depth) & (n == LANES - 1))
    minus = ((k < LANES) & (k == n - 1)) | ((beyond >= 0) & (beyond < depth) & (n == 0))
    across[...] = (plus.astype(jnp.float32) - minus.astype(jnp.float32)).astype(jnp.bfloat16)
    z_of = lax.broadcasted_iota(jnp.int32, (depth, STRIP, LANES), 0)
    lane_of = lax.broadcasted_iota(jnp.int32, (depth, STRIP, LANES), 2)
    own = (lane_of == z_of) | (lane_of == z_of + depth)
    picked[...] = own.astype(jnp.float32).astype(jnp.bfloat16)

    load.wait()

    lane = lax.broadcasted_iota(jnp.int32, (STRIP, LANES), 1)

    def gather_edges(s, carry):
        packed = jnp.zeros((STRIP, LANES), jnp.float32)
        at = pl.ds(pl.multiple_of(STRIP + s * STRIP, STRIP), STRIP)
        for z in range(depth):
            row = cells[1 + z, at].astype(jnp.float32)
            packed = jnp.where(lane == z, pltpu.roll(row, z + 1, 1), packed)
            packed = jnp.where(lane == depth + z, pltpu.roll(row, depth + z, 1), packed)
        edges[pl.ds(pl.multiple_of(s * STRIP, STRIP), STRIP)] = packed.astype(jnp.bfloat16)
        return carry

    lax.fori_loop(0, height // STRIP, gather_edges, 0)
    for i in range(4, 6):

        @pl.when(beside[i][0])
        def _():
            copies[i].start()

    for i in range(6):

        @pl.when(beside[i ^ 1][0])
        def _():
            copies[i].wait_recv()

    def partial_image(s):
        window = pl.ds(pl.multiple_of(s * STRIP, STRIP), 3 * STRIP)
        inner = pl.ds(pl.multiple_of(s * STRIP + STRIP, STRIP), STRIP)
        at = pl.ds(pl.multiple_of(s * STRIP, STRIP), STRIP)
        outside = jnp.where(lane < depth, edges_left[at].astype(jnp.float32), edges_right[at].astype(jnp.float32))
        outside = outside.astype(jnp.bfloat16)[None] * picked[...]
        middle = cells[pl.ds(1, depth), inner]
        left_hand = jnp.concatenate(
            [middle.reshape(depth * STRIP, LANES), outside.reshape(depth * STRIP, LANES)], axis=1
        )
        diff_x = jnp.dot(left_hand, across[...], preferred_element_type=jnp.float32)
        colour = [[jnp.zeros((HALF, LANES), jnp.float32)] * 3 for _ in range(2)]
        through = [jnp.ones((HALF, LANES), jnp.float32) for _ in range(2)]
        behind = cells[0, inner].astype(jnp.float32)
        here = cells[1, window].astype(jnp.float32)
        for z in range(depth):
            if z + 1 < depth:
                ahead_rows = cells[z + 2, window].astype(jnp.float32)
                ahead = ahead_rows[STRIP : 2 * STRIP]
            else:
                ahead_rows = None
                ahead = cells[z + 2, inner].astype(jnp.float32)
            near = here[HALF : 5 * HALF]
            diff_y = pltpu.roll(near, 4 * HALF - 1, 0) - pltpu.roll(near, 1, 0)
            diff_y = diff_y[HALF : 3 * HALF]
            centre_rows = here[STRIP : 2 * STRIP]
            diff_z = ahead - behind
            for h in range(2):
                part = slice(h * HALF, (h + 1) * HALF)
                gz, gy = diff_z[part], diff_y[part]
                gx = diff_x[z * STRIP + h * HALF : z * STRIP + (h + 1) * HALF]
                value = centre_rows[part]
                root = lax.rsqrt(gz * gz + gy * gy + gx * gx + 4.0)
                lit = jnp.abs(DIFFUSE * LIGHT_Z * gz + DIFFUSE * LIGHT_Y * gy + DIFFUSE * LIGHT_X * gx)
                shading = AMBIENT + lit * root
                scale = (knots - 1) / (VALUE_HIGH - VALUE_LOW)
                scaled = jnp.clip(value * scale - VALUE_LOW * scale, 0.0, knots - 1.0)
                index = scaled.astype(jnp.int32)
                red, green, blue, extinction = [
                    look_up(base, index) + look_up(slope, index) * scaled for base, slope in tables
                ]
                passed = jnp.exp2(extinction * (0.3 - root * root))
                after = through[h] * passed
                weight = (through[h] - after) * shading
                through[h] = after
                for channel, value_of in enumerate((red, green, blue)):
                    colour[h][channel] = colour[h][channel] + value_of * weight
            behind, here = centre_rows, ahead_rows
        return [
            jnp.concatenate([colour[0][0], colour[1][0]], axis=0),
            jnp.concatenate([colour[0][1], colour[1][1]], axis=0),
            jnp.concatenate([colour[0][2], colour[1][2]], axis=0),
            1.0 - jnp.concatenate(through, axis=0),
        ]

    def send_to(s):
        return pltpu.make_async_remote_copy(
            src_ref=outgoing.at[s],
            dst_ref=arrived.at[v],
            send_sem=part_send.at[s],
            recv_sem=part_recv.at[v],
            device_id={"view": s},
            device_id_type=MESH,
        )

    def work(step, carry):
        offset = jnp.where(step % 2 == 0, views // 2 - step // 2, views // 2 + (step + 1) // 2)
        s = lax.rem(v + offset, views)
        image = partial_image(s)
        for channel in range(4):
            outgoing[s, channel] = image[channel].astype(jnp.bfloat16)

        @pl.when(s != v)
        def _():
            send_to(s).start()

        return carry

    lax.fori_loop(0, views, work, 0)

    for i in range(6):

        @pl.when(beside[i][0])
        def _():
            copies[i].wait_send()

    arrived[v] = outgoing[v]
    image = [jnp.zeros((STRIP, LANES), jnp.float32)] * 3
    through = jnp.ones((STRIP, LANES), jnp.float32)
    for source in range(views):

        @pl.when(v != source)
        def _():
            pltpu.make_async_remote_copy(
                src_ref=outgoing.at[source],
                dst_ref=arrived.at[source],
                send_sem=part_send.at[source],
                recv_sem=part_recv.at[source],
                device_id={"view": source},
                device_id_type=MESH,
            ).wait()

        layer = arrived[source].astype(jnp.float32)
        for channel in range(3):
            image[channel] = image[channel] + through * layer[channel]
        through = through * (1.0 - layer[3])
    for channel in range(3):
        out_ref[channel, 0] = image[channel]
    out_ref[3, 0] = 1.0 - through


def solution(mesh):
    counts = tuple(mesh.shape[axis] for axis in ("view", "row", "col"))

    def on_device(volume, tf_color, tf_opacity):
        depth, height, width = volume.shape
        views = counts[0]
        half = jnp.bfloat16
        return pl.pallas_call(
            lambda *refs: kernel(counts, *refs),
            name="render",
            out_shape=jax.ShapeDtypeStruct((4, 1, height // views, width), jnp.float32),
            in_specs=[
                pl.BlockSpec(memory_space=pl.ANY),
                pl.BlockSpec(memory_space=pltpu.SMEM),
                pl.BlockSpec(memory_space=pltpu.SMEM),
            ],
            out_specs=pl.BlockSpec(memory_space=pltpu.VMEM),
            scratch_shapes=[
                pltpu.VMEM((depth + 2, height + 2 * STRIP, width), half),
                pltpu.VMEM((height, width), half),
                pltpu.VMEM((height, width), half),
                pltpu.VMEM((height, width), half),
                pltpu.VMEM((2 * width, width), half),
                pltpu.VMEM((depth, STRIP, width), half),
                pltpu.VMEM((views, 4, STRIP, width), half),
                pltpu.VMEM((views, 4, STRIP, width), half),
                pltpu.SemaphoreType.DMA,
                pltpu.SemaphoreType.DMA((6,)),
                pltpu.SemaphoreType.DMA((6,)),
                pltpu.SemaphoreType.DMA((views,)),
                pltpu.SemaphoreType.DMA((views,)),
            ],
            compiler_params=pltpu.CompilerParams(collective_id=0, has_side_effects=True),
        )(volume, tf_color, tf_opacity)

    return jax.shard_map(
        on_device,
        mesh=mesh,
        in_specs=(P("view", "row", "col"), P(), P()),
        out_specs=P(None, "view", "row", "col"),
        check_vma=False,
    )
```

time: 151 us -> 27 us (0.18)
  the two profiles are of different devices: /device:TPU:1 before, /device:TPU:199 now
where the time goes in v1:
time: 27 us; the launch traced here: 26.8 us
  Pallas kernels  25.4 us (94%)
  local copies, waits for them, and re-layouts  1.38 us (5%)
    pallas_call x1, Pallas kernels, on_device(): pl.pallas_call(lambda *refs: kernel(counts, *refs), name='render', out_sh...  25.4 us
    unnamed x1, local copies, waits for them, and re-layouts  1.38 us

profile of v1, /device:TPU:199, one launch (start us, length us, event | category | flops | bytes accessed | tf_op | source)
XLA Modules:
  0.0 26.8 jit_solution(5223967784296046193)
XLA Ops:
  0.0 25.4 %render.1 = f32[4,1,16,128]{3,2,1,0:T(8,128)} custom-call(bf16[16,256,128]{2,1,0:T(8,128)(2,1)} %refs_0_.1, f32[3,16]{1,0:T(4,128)} %refs_1_.1, f32[16]{0:T(128)} %refs_2_.1), custom_call_target="tpu_custom_call" | custom-call | tf_op jit(solution)/shard_map/render/pallas_call | solution.py:291
  25.4 1.4 %copy.5 = f32[4,1,16,128]{3,2,1,0:T(8,128)} copy(f32[4,1,16,128]{3,2,1,0:T(8,128)} %render.1) | data formatting | bytes 65536

commit v2 on v1

v2 whole, which is shorter than its diff:
```python
import math

import jax
import jax.numpy as jnp
from jax import lax
from jax.experimental import pallas as pl
from jax.experimental.pallas import tpu as pltpu
from jax.sharding import PartitionSpec as P

LIGHT_Z = 0.48
LIGHT_Y = 0.6
LIGHT_X = 0.64
VALUE_LOW = -3.0
VALUE_HIGH = 3.0
AMBIENT = 0.35
DIFFUSE = 0.65

MESH = pl.DeviceIdType.MESH
LANES = 128
STRIP = 16
HALF = 8
CORES = 2


def tables_of(color_ref, opacity_ref, knots, scales):
    row = lax.broadcasted_iota(jnp.int32, (HALF, LANES), 0)
    lane = lax.broadcasted_iota(jnp.int32, (HALF, LANES), 1)
    pairs = []
    for channel in range(4):
        at_knot = [
            (color_ref[channel, k] if channel < 3 else opacity_ref[k]) * scales[channel] for k in range(knots)
        ]
        odd = jnp.zeros((HALF, LANES), jnp.float32)
        slope = jnp.zeros((HALF, LANES), jnp.float32)
        for k in range(1, knots, 2):
            odd = jnp.where(row == k // 2, at_knot[k], odd)
        for k in range(knots - 1):
            slope = jnp.where(lane == k, at_knot[k + 1] - at_knot[k], slope)
        pairs.append((odd, slope))
    return pairs


def look_up(table, index, axis):
    other = 1 - axis
    dims = lax.GatherDimensionNumbers(
        offset_dims=(),
        collapsed_slice_dims=(axis,),
        start_index_map=(axis,),
        operand_batching_dims=(other,),
        start_indices_batching_dims=(other,),
    )
    mode = lax.GatherScatterMode.PROMISE_IN_BOUNDS
    return lax.gather(table, index[..., None], dims, slice_sizes=(1, 1), mode=mode)


def kernel(
    counts,
    volume,
    color_ref,
    opacity_ref,
    out_ref,
    cells,
    wide,
    edges,
    edges_left,
    edges_right,
    across,
    picked,
    parts,
    theirs,
    outgoing,
    arrived,
    load_sem,
    halo_send,
    halo_recv,
    swap_send,
    swap_recv,
    part_send,
    part_recv,
):
    views, rows, cols = counts
    chips = views // CORES
    depth, height, _ = volume.shape
    knots = color_ref.shape[1]
    groups = LANES // (2 * depth)
    group_rows = height // groups
    v, r, c = lax.axis_index("view"), lax.axis_index("row"), lax.axis_index("col")
    core, chip = lax.rem(v, CORES), v // CORES
    partner = v + 1 - 2 * core
    body = pl.ds(STRIP, height)

    load = pltpu.make_async_copy(volume, cells.at[pl.ds(1, depth), body], load_sem)
    load.start()

    beside = [
        (v > 0, {"view": v - 1}),
        (v < views - 1, {"view": v + 1}),
        (r > 0, {"row": r - 1}),
        (r < rows - 1, {"row": r + 1}),
        (c > 0, {"col": c - 1}),
        (c < cols - 1, {"col": c + 1}),
    ]
    barrier = pltpu.get_barrier_semaphore()
    expected = chips - 1
    for there, where in beside:
        expected = expected + there.astype(jnp.int32)

        @pl.when(there)
        def _():
            pl.semaphore_signal(barrier, inc=1, device_id=where, device_id_type=MESH)

    for step in range(1, chips):
        other = lax.rem(v + CORES * step, views)
        pl.semaphore_signal(barrier, inc=1, device_id={"view": other}, device_id_type=MESH)

    group_of = lax.broadcasted_iota(jnp.int32, (groups * depth, STRIP, LANES), 0)
    lane_of = lax.broadcasted_iota(jnp.int32, (groups * depth, STRIP, LANES), 2)
    first_lane = group_of + (group_of // depth) * depth
    own = (lane_of == first_lane) | (lane_of == first_lane + depth)
    picked[...] = own.astype(jnp.float32).astype(jnp.bfloat16)

    pl.semaphore_wait(barrier, expected)

    sources = [
        volume.at[pl.ds(0, 1)],
        volume.at[pl.ds(depth - 1, 1)],
        volume.at[:, pl.ds(0, STRIP)],
        volume.at[:, pl.ds(height - STRIP, STRIP)],
        edges,
        edges,
    ]
    landings = [
        cells.at[pl.ds(depth + 1, 1), body],
        cells.at[pl.ds(0, 1), body],
        cells.at[pl.ds(1, depth), pl.ds(STRIP + height, STRIP)],
        cells.at[pl.ds(1, depth), pl.ds(0, STRIP)],
        edges_right,
        edges_left,
    ]
    copies = [
        pltpu.make_async_remote_copy(
            src_ref=sources[i],
            dst_ref=landings[i],
            send_sem=halo_send.at[i],
            recv_sem=halo_recv.at[i],
            device_id=beside[i][1],
            device_id_type=MESH,
        )
        for i in range(6)
    ]
    for i in range(4):

        @pl.when(beside[i][0])
        def _():
            copies[i].start()

    load.wait()

    narrow = lax.broadcasted_iota(jnp.int32, (STRIP, LANES), 1)
    from_left = (narrow & (2 * depth - 1)) < depth
    taken = jnp.where(from_left, LANES - 1, 0).astype(jnp.int16)
    for b in range(group_rows // STRIP):
        packed = jnp.zeros((STRIP, LANES), jnp.bfloat16)
        for g in range(groups):
            for z in range(depth):
                row = cells[1 + z, pl.ds(STRIP + g * group_rows + b * STRIP, STRIP)]
                packed = packed + look_up(row, taken, 1) * picked[g * depth + z]
        edges[pl.ds(b * STRIP, STRIP)] = packed
    for i in range(4, 6):

        @pl.when(beside[i][0])
        def _():
            copies[i].start()

    for i in range(6):

        @pl.when(jnp.logical_not(beside[i ^ 1][0]))
        def _():
            landings[i][...] = jnp.zeros(landings[i].shape, landings[i].dtype)

    light = DIFFUSE * LIGHT_Z
    scales = [light] * 3 + [-8.0 * math.log2(math.e) / (depth * views)]
    tables = tables_of(color_ref, opacity_ref, knots, scales)

    k = lax.broadcasted_iota(jnp.int32, (2 * LANES, LANES), 0)
    n = lax.broadcasted_iota(jnp.int32, (2 * LANES, LANES), 1)
    inside = k < LANES
    place = k & (2 * depth - 1)
    plus = (inside & (k == n + 1)) | ((k >= LANES) & (place >= depth) & (n == LANES - 1))
    minus = (inside & (k == n - 1)) | ((k >= LANES) & (place < depth) & (n == 0))
    across[...] = (plus.astype(jnp.float32) - minus.astype(jnp.float32)).astype(jnp.bfloat16)

    def widen(s, carry):
        for z in range(depth):
            some = cells[1 + z, pl.ds(pl.multiple_of(STRIP + s * STRIP, STRIP), STRIP)]
            wide[z, pl.ds(pl.multiple_of(HALF + s * STRIP, HALF), STRIP)] = some.astype(jnp.float32)
        return carry

    lax.fori_loop(0, height // STRIP, widen, 0)

    for i in range(6):

        @pl.when(beside[i ^ 1][0])
        def _():
            copies[i].wait_recv()

    for z in range(depth):
        wide[z, pl.ds(0, HALF)] = cells[1 + z, pl.ds(0, STRIP)].astype(jnp.float32)[HALF:]
        wide[z, pl.ds(HALF + height, HALF)] = cells[1 + z, pl.ds(STRIP + height, STRIP)].astype(jnp.float32)[:HALF]

    def partial_image(s):
        inner = pl.ds(pl.multiple_of(s * STRIP + STRIP, STRIP), STRIP)
        b = pl.ds(pl.multiple_of(lax.rem(s * STRIP, group_rows), STRIP), STRIP)
        outside = jnp.where(from_left, edges_left[b].astype(jnp.float32), edges_right[b].astype(jnp.float32))
        mine = picked[pl.ds((s * STRIP // group_rows) * depth, depth)]
        outside = outside.astype(jnp.bfloat16)[None] * mine
        middle = cells[pl.ds(1, depth), inner]
        left_hand = jnp.concatenate(
            [middle.reshape(depth * STRIP, LANES), outside.reshape(depth * STRIP, LANES)], axis=1
        )
        diff_x = jnp.dot(left_hand, across[...], preferred_element_type=jnp.float32)
        colour = [[jnp.zeros((HALF, LANES), jnp.float32)] * 3 for _ in range(2)]
        through = [jnp.ones((HALF, LANES), jnp.float32) for _ in range(2)]
        first = cells[0, inner].astype(jnp.float32)
        last = cells[depth + 1, inner].astype(jnp.float32)
        for z in range(depth):
            for h in range(2):
                base = pl.multiple_of(s * STRIP, STRIP) + h * HALF
                part = slice(h * HALF, (h + 1) * HALF)
                here = pl.ds(base + HALF, HALF)
                value = wide[z, here]
                behind = wide[z - 1, here] if z > 0 else first[part]
                ahead = wide[z + 1, here] if z + 1 < depth else last[part]
                gz = ahead - behind
                gy = wide[z, pl.ds(base + HALF + 1, HALF)] - wide[z, pl.ds(base + HALF - 1, HALF)]
                gx = diff_x[z * STRIP + h * HALF : z * STRIP + (h + 1) * HALF]
                root = lax.rsqrt(gz * gz + gy * gy + (gx * gx + 4.0))
                lit = jnp.abs(gz + (LIGHT_Y / LIGHT_Z) * gy + (LIGHT_X / LIGHT_Z) * gx)
                shading = AMBIENT / light + lit * root
                scale = (knots - 1) / (VALUE_HIGH - VALUE_LOW)
                scaled = jnp.clip(value * scale - VALUE_LOW * scale, 0.0, knots - 1.0)
                interval = scaled.astype(jnp.int32)
                pair = lax.shift_right_logical(interval, 1)
                away = scaled - (interval | 1).astype(jnp.float32)
                red, green, blue, extinction = [
                    look_up(odd, pair, 0) + look_up(slope, interval, 1) * away for odd, slope in tables
                ]
                passed = jnp.exp2(extinction * (0.3 - root * root))
                after = through[h] * passed
                weight = (through[h] - after) * shading
                through[h] = after
                for channel, value_of in enumerate((red, green, blue)):
                    colour[h][channel] = colour[h][channel] + value_of * weight
        return [jnp.concatenate([colour[0][i], colour[1][i]], axis=0) for i in range(3)] + [
            jnp.concatenate(through, axis=0)
        ]

    def chip_of(i):
        ahead = jnp.where(i % 2 == 0, chips // 2 - i // 2, chips // 2 + (i + 1) // 2)
        return lax.rem(chip + ahead, chips)

    def swap(i):
        return pltpu.make_async_remote_copy(
            src_ref=parts.at[i],
            dst_ref=theirs.at[i],
            send_sem=swap_send.at[i],
            recv_sem=swap_recv.at[i],
            device_id={"view": partner},
            device_id_type=MESH,
        )

    def hand_over(to_chip, from_chip):
        return pltpu.make_async_remote_copy(
            src_ref=outgoing.at[to_chip],
            dst_ref=arrived.at[from_chip],
            send_sem=part_send.at[to_chip],
            recv_sem=part_recv.at[from_chip],
            device_id={"view": CORES * to_chip + core},
            device_id_type=MESH,
        )

    def work(step, carry):
        i = lax.rem(step, chips)
        late = step // chips
        to_chip = chip_of(i)
        s = CORES * to_chip + jnp.where(late == 1, core, 1 - core)
        image = partial_image(s)
        for channel in range(4):
            parts[step, channel] = image[channel]

        @pl.when(late == 0)
        def _():
            swap(i).start()

        @pl.when(late == 1)
        def _():
            swap(i).wait_recv()
            front, back = [], []
            for channel in range(4):
                a, b = parts[step, channel], theirs[i, channel]
                front.append(jnp.where(core == 0, a, b))
                back.append(jnp.where(core == 0, b, a))
            for channel in range(3):
                outgoing[to_chip, channel] = (front[channel] + front[3] * back[channel]).astype(jnp.bfloat16)
            outgoing[to_chip, 3] = (1.0 - front[3] * back[3]).astype(jnp.bfloat16)

            @pl.when(to_chip != chip)
            def _():
                hand_over(to_chip, chip).start()

        return carry

    lax.fori_loop(0, views, work, 0)

    for i in range(6):

        @pl.when(beside[i][0])
        def _():
            copies[i].wait_send()

    for i in range(chips):
        swap(i).wait_send()

    arrived[chip] = outgoing[chip]
    image = [jnp.zeros((STRIP, LANES), jnp.float32)] * 3
    through = jnp.ones((STRIP, LANES), jnp.float32)
    for source in range(chips):

        @pl.when(chip != source)
        def _():
            hand_over(source, source).wait()

        layer = arrived[source].astype(jnp.float32)
        for channel in range(3):
            image[channel] = image[channel] + through * layer[channel]
        through = through * (1.0 - layer[3])
    for channel in range(3):
        out_ref[channel, 0] = image[channel]
    out_ref[3, 0] = 1.0 - through


def solution(mesh):
    counts = tuple(mesh.shape[axis] for axis in ("view", "row", "col"))

    def on_device(volume, tf_color, tf_opacity):
        depth, height, width = volume.shape
        views = counts[0]
        chips = views // CORES
        half, full = jnp.bfloat16, jnp.float32
        edge_rows = height * 2 * depth // LANES
        return pl.pallas_call(
            lambda *refs: kernel(counts, *refs),
            name="render",
            out_shape=jax.ShapeDtypeStruct((4, 1, height // views, width), jnp.float32),
            in_specs=[
                pl.BlockSpec(memory_space=pltpu.HBM),
                pl.BlockSpec(memory_space=pltpu.SMEM),
                pl.BlockSpec(memory_space=pltpu.SMEM),
            ],
            out_specs=pl.BlockSpec(memory_space=pltpu.VMEM),
            scratch_shapes=[
                pltpu.VMEM((depth + 2, height + 2 * STRIP, width), half),
                pltpu.VMEM((depth, height + 2 * HALF, width), full),
                pltpu.VMEM((edge_rows, width), half),
                pltpu.VMEM((edge_rows, width), half),
                pltpu.VMEM((edge_rows, width), half),
                pltpu.VMEM((2 * width, width), half),
                pltpu.VMEM((LANES // 2, STRIP, width), half),
                pltpu.VMEM((views, 4, STRIP, width), full),
                pltpu.VMEM((chips, 4, STRIP, width), full),
                pltpu.VMEM((chips, 4, STRIP, width), half),
                pltpu.VMEM((chips, 4, STRIP, width), half),
                pltpu.SemaphoreType.DMA,
                pltpu.SemaphoreType.DMA((6,)),
                pltpu.SemaphoreType.DMA((6,)),
                pltpu.SemaphoreType.DMA((chips,)),
                pltpu.SemaphoreType.DMA((chips,)),
                pltpu.SemaphoreType.DMA((chips,)),
                pltpu.SemaphoreType.DMA((chips,)),
            ],
            compiler_params=pltpu.CompilerParams(collective_id=0, has_side_effects=True),
        )(volume, tf_color, tf_opacity)

    return jax.shard_map(
        on_device,
        mesh=mesh,
        in_specs=(P("view", "row", "col"), P(), P()),
        out_specs=P(None, "view", "row", "col"),
        check_vma=False,
    )
```

time: 27 us -> 24.5 us (0.907)
  the two profiles are of different devices: /device:TPU:199 before, /device:TPU:1 now
where the time goes in v2:
time: 24.5 us; the launch traced here: 24.2 us
  Pallas kernels  22.8 us (93%)
  local copies, waits for them, and re-layouts  1.38 us (6%)
    pallas_call x1, Pallas kernels, on_device(): pl.pallas_call(lambda *refs: kernel(counts, *refs), name='render', out_sh...  22.8 us
    unnamed x1, local copies, waits for them, and re-layouts  1.38 us

profile of v2, /device:TPU:1, one launch (start us, length us, event | category | flops | bytes accessed | tf_op | source)
XLA Modules:
  0.0 24.2 jit_solution(3458966154480642070)
XLA Ops:
  0.0 22.8 %render.1 = f32[4,1,16,128]{3,2,1,0:T(8,128)} custom-call(bf16[16,256,128]{2,1,0:T(8,128)(2,1)} %refs_0_.1, f32[3,16]{1,0:T(4,128)} %refs_1_.1, f32[16]{0:T(128)} %refs_2_.1), custom_call_target="tpu_custom_call" | custom-call | tf_op jit(solution)/shard_map/render/pallas_call | solution.py:351
  22.9 1.4 %copy.5 = f32[4,1,16,128]{3,2,1,0:T(8,128)} copy(f32[4,1,16,128]{3,2,1,0:T(8,128)} %render.1) | data formatting | bytes 65536

commit v3 on v2

--- a/solution.py
+++ b/solution.py
@@ -56,21 +56,27 @@
 def kernel(
     counts,
     volume,
+    color_hbm,
+    opacity_hbm,
+    out_ref,
     color_ref,
     opacity_ref,
-    out_ref,
     cells,
     wide,
     edges,
     edges_left,
     edges_right,
     across,
+    diff_even,
+    diff_odd,
     picked,
     parts,
     theirs,
     outgoing,
     arrived,
     load_sem,
+    table_sem,
+    ready_sem,
     halo_send,
     halo_recv,
     swap_send,
@@ -91,6 +97,12 @@
 
     load = pltpu.make_async_copy(volume, cells.at[pl.ds(1, depth), body], load_sem)
     load.start()
+    loads = [
+        pltpu.make_async_copy(color_hbm, color_ref, table_sem.at[0]),
+        pltpu.make_async_copy(opacity_hbm, opacity_ref, table_sem.at[1]),
+    ]
+    for one in loads:
+        one.start()
 
     beside = [
         (v > 0, {"view": v - 1}),
@@ -101,7 +113,7 @@
         (c < cols - 1, {"col": c + 1}),
     ]
     barrier = pltpu.get_barrier_semaphore()
-    expected = chips - 1
+    expected = 0
     for there, where in beside:
         expected = expected + there.astype(jnp.int32)
 
@@ -109,9 +121,13 @@
         def _():
             pl.semaphore_signal(barrier, inc=1, device_id=where, device_id_type=MESH)
 
-    for step in range(1, chips):
-        other = lax.rem(v + CORES * step, views)
-        pl.semaphore_signal(barrier, inc=1, device_id={"view": other}, device_id_type=MESH)
+    def greet(semaphore, distance):
+        for way in sorted({distance, chips - distance}):
+            other = lax.rem(v + CORES * way, views)
+            pl.semaphore_signal(semaphore, inc=1, device_id={"view": other}, device_id_type=MESH)
+        return len({distance, chips - distance})
+
+    expected = expected + greet(barrier, 1)
 
     group_of = lax.broadcasted_iota(jnp.int32, (groups * depth, STRIP, LANES), 0)
     lane_of = lax.broadcasted_iota(jnp.int32, (groups * depth, STRIP, LANES), 2)
@@ -154,6 +170,9 @@
         def _():
             copies[i].start()
 
+    rounds = max(chips // 2 - 1, 0).bit_length()
+    heard = [greet(ready_sem.at[0], 1)] if rounds > 0 else []
+
     load.wait()
 
     narrow = lax.broadcasted_iota(jnp.int32, (STRIP, LANES), 1)
@@ -172,14 +191,26 @@
         def _():
             copies[i].start()
 
+    for k in range(1, rounds):
+        pl.semaphore_wait(ready_sem.at[k - 1], heard[-1])
+        heard.append(greet(ready_sem.at[k], 2**k))
+
     for i in range(6):
 
         @pl.when(jnp.logical_not(beside[i ^ 1][0]))
         def _():
             landings[i][...] = jnp.zeros(landings[i].shape, landings[i].dtype)
 
+    scale = (knots - 1) / (VALUE_HIGH - VALUE_LOW)
+    square = (2.0 * scale) ** 2
     light = DIFFUSE * LIGHT_Z
-    scales = [light] * 3 + [-8.0 * math.log2(math.e) / (depth * views)]
+    scales = [light] * 3 + [-2.0 * square * math.log2(math.e) / (depth * views)]
+
+    def placed(some):
+        return some.astype(jnp.float32) * scale - VALUE_LOW * scale
+
+    for one in loads:
+        one.wait()
     tables = tables_of(color_ref, opacity_ref, knots, scales)
 
     k = lax.broadcasted_iota(jnp.int32, (2 * LANES, LANES), 0)
@@ -188,12 +219,12 @@
     place = k & (2 * depth - 1)
     plus = (inside & (k == n + 1)) | ((k >= LANES) & (place >= depth) & (n == LANES - 1))
     minus = (inside & (k == n - 1)) | ((k >= LANES) & (place < depth) & (n == 0))
-    across[...] = (plus.astype(jnp.float32) - minus.astype(jnp.float32)).astype(jnp.bfloat16)
+    across[...] = ((plus.astype(jnp.float32) - minus.astype(jnp.float32)) * scale).astype(jnp.bfloat16)
 
     def widen(s, carry):
         for z in range(depth):
             some = cells[1 + z, pl.ds(pl.multiple_of(STRIP + s * STRIP, STRIP), STRIP)]
-            wide[z, pl.ds(pl.multiple_of(HALF + s * STRIP, HALF), STRIP)] = some.astype(jnp.float32)
+            wide[z, pl.ds(pl.multiple_of(HALF + s * STRIP, HALF), STRIP)] = placed(some)
         return carry
 
     lax.fori_loop(0, height // STRIP, widen, 0)
@@ -205,10 +236,12 @@
             copies[i].wait_recv()
 
     for z in range(depth):
-        wide[z, pl.ds(0, HALF)] = cells[1 + z, pl.ds(0, STRIP)].astype(jnp.float32)[HALF:]
-        wide[z, pl.ds(HALF + height, HALF)] = cells[1 + z, pl.ds(STRIP + height, STRIP)].astype(jnp.float32)[:HALF]
-
-    def partial_image(s):
+        wide[z, pl.ds(0, HALF)] = placed(cells[1 + z, pl.ds(0, STRIP)])[HALF:]
+        wide[z, pl.ds(HALF + height, HALF)] = placed(cells[1 + z, pl.ds(STRIP + height, STRIP)])[:HALF]
+    if rounds > 0:
+        pl.semaphore_wait(ready_sem.at[rounds - 1], heard[-1])
+
+    def difference_x(s):
         inner = pl.ds(pl.multiple_of(s * STRIP + STRIP, STRIP), STRIP)
         b = pl.ds(pl.multiple_of(lax.rem(s * STRIP, group_rows), STRIP), STRIP)
         outside = jnp.where(from_left, edges_left[b].astype(jnp.float32), edges_right[b].astype(jnp.float32))
@@ -218,11 +251,14 @@
         left_hand = jnp.concatenate(
             [middle.reshape(depth * STRIP, LANES), outside.reshape(depth * STRIP, LANES)], axis=1
         )
-        diff_x = jnp.dot(left_hand, across[...], preferred_element_type=jnp.float32)
+        return jnp.dot(left_hand, across[...], preferred_element_type=jnp.float32)
+
+    def partial_image(s, diff):
+        inner = pl.ds(pl.multiple_of(s * STRIP + STRIP, STRIP), STRIP)
         colour = [[jnp.zeros((HALF, LANES), jnp.float32)] * 3 for _ in range(2)]
         through = [jnp.ones((HALF, LANES), jnp.float32) for _ in range(2)]
-        first = cells[0, inner].astype(jnp.float32)
-        last = cells[depth + 1, inner].astype(jnp.float32)
+        first = placed(cells[0, inner])
+        last = placed(cells[depth + 1, inner])
         for z in range(depth):
             for h in range(2):
                 base = pl.multiple_of(s * STRIP, STRIP) + h * HALF
@@ -233,19 +269,18 @@
                 ahead = wide[z + 1, here] if z + 1 < depth else last[part]
                 gz = ahead - behind
                 gy = wide[z, pl.ds(base + HALF + 1, HALF)] - wide[z, pl.ds(base + HALF - 1, HALF)]
-                gx = diff_x[z * STRIP + h * HALF : z * STRIP + (h + 1) * HALF]
-                root = lax.rsqrt(gz * gz + gy * gy + (gx * gx + 4.0))
+                gx = diff[pl.ds(z * STRIP + h * HALF, HALF)]
+                root = lax.rsqrt(gz * gz + gy * gy + (gx * gx + square))
                 lit = jnp.abs(gz + (LIGHT_Y / LIGHT_Z) * gy + (LIGHT_X / LIGHT_Z) * gx)
                 shading = AMBIENT / light + lit * root
-                scale = (knots - 1) / (VALUE_HIGH - VALUE_LOW)
-                scaled = jnp.clip(value * scale - VALUE_LOW * scale, 0.0, knots - 1.0)
+                scaled = jnp.clip(value, 0.0, knots - 1.0)
                 interval = scaled.astype(jnp.int32)
                 pair = lax.shift_right_logical(interval, 1)
                 away = scaled - (interval | 1).astype(jnp.float32)
                 red, green, blue, extinction = [
                     look_up(odd, pair, 0) + look_up(slope, interval, 1) * away for odd, slope in tables
                 ]
-                passed = jnp.exp2(extinction * (0.3 - root * root))
+                passed = jnp.exp2(extinction * (1.2 / square - root * root))
                 after = through[h] * passed
                 weight = (through[h] - after) * shading
                 through[h] = after
@@ -279,38 +314,51 @@
             device_id_type=MESH,
         )
 
-    def work(step, carry):
-        i = lax.rem(step, chips)
-        late = step // chips
-        to_chip = chip_of(i)
-        s = CORES * to_chip + jnp.where(late == 1, core, 1 - core)
-        image = partial_image(s)
-        for channel in range(4):
-            parts[step, channel] = image[channel]
-
-        @pl.when(late == 0)
-        def _():
+    def strip_of(step):
+        side = jnp.where(step < chips, 1 - core, core)
+        return CORES * chip_of(lax.rem(step, chips)) + side
+
+    diff_even[...] = difference_x(strip_of(0))
+
+    def give(t, carry):
+        for odd, diff, following in ((0, diff_even, diff_odd), (1, diff_odd, diff_even)):
+            i = 2 * t + odd
+            following[...] = difference_x(strip_of(i + 1))
+            image = partial_image(strip_of(i), diff)
+            for channel in range(4):
+                parts[i, channel] = image[channel]
             swap(i).start()
-
-        @pl.when(late == 1)
-        def _():
-            swap(i).wait_recv()
+        return carry
+
+    lax.fori_loop(0, chips // 2, give, 0)
+
+    def merge(t, carry):
+        for odd in range(2):
+            swap(2 * t + odd).wait_recv()
+        for odd, diff, following in ((0, diff_even, diff_odd), (1, diff_odd, diff_even)):
+            i = 2 * t + odd
+            to_chip = chip_of(i)
+            following[...] = difference_x(strip_of(lax.rem(chips + i + 1, views)))
+            image = partial_image(strip_of(chips + i), diff)
             front, back = [], []
             for channel in range(4):
-                a, b = parts[step, channel], theirs[i, channel]
-                front.append(jnp.where(core == 0, a, b))
-                back.append(jnp.where(core == 0, b, a))
+                other = theirs[i, channel]
+                front.append(jnp.where(core == 0, image[channel], other))
+                back.append(jnp.where(core == 0, other, image[channel]))
             for channel in range(3):
                 outgoing[to_chip, channel] = (front[channel] + front[3] * back[channel]).astype(jnp.bfloat16)
             outgoing[to_chip, 3] = (1.0 - front[3] * back[3]).astype(jnp.bfloat16)
-
-            @pl.when(to_chip != chip)
-            def _():
+            if odd == 0:
                 hand_over(to_chip, chip).start()
+            else:
+
+                @pl.when(to_chip != chip)
+                def _():
+                    hand_over(to_chip, chip).start()
 
         return carry
 
-    lax.fori_loop(0, views, work, 0)
+    lax.fori_loop(0, chips // 2, merge, 0)
 
     for i in range(6):
 
@@ -353,24 +401,30 @@
             name="render",
             out_shape=jax.ShapeDtypeStruct((4, 1, height // views, width), jnp.float32),
             in_specs=[
-                pl.BlockSpec(memory_space=pltpu.HBM),
-                pl.BlockSpec(memory_space=pltpu.SMEM),
-                pl.BlockSpec(memory_space=pltpu.SMEM),
+                pl.BlockSpec(memory_space=pl.ANY),
+                pl.BlockSpec(memory_space=pl.ANY),
+                pl.BlockSpec(memory_space=pl.ANY),
             ],
             out_specs=pl.BlockSpec(memory_space=pltpu.VMEM),
             scratch_shapes=[
+                pltpu.SMEM(tf_color.shape, full),
+                pltpu.SMEM(tf_opacity.shape, full),
                 pltpu.VMEM((depth + 2, height + 2 * STRIP, width), half),
                 pltpu.VMEM((depth, height + 2 * HALF, width), full),
                 pltpu.VMEM((edge_rows, width), half),
                 pltpu.VMEM((edge_rows, width), half),
                 pltpu.VMEM((edge_rows, width), half),
                 pltpu.VMEM((2 * width, width), half),
+                pltpu.VMEM((depth * STRIP, width), full),
+                pltpu.VMEM((depth * STRIP, width), full),
                 pltpu.VMEM((LANES // 2, STRIP, width), half),
-                pltpu.VMEM((views, 4, STRIP, width), full),
+                pltpu.VMEM((chips, 4, STRIP, width), full),
                 pltpu.VMEM((chips, 4, STRIP, width), full),
                 pltpu.VMEM((chips, 4, STRIP, width), half),
                 pltpu.VMEM((chips, 4, STRIP, width), half),
                 pltpu.SemaphoreType.DMA,
+                pltpu.SemaphoreType.DMA((2,)),
+                pltpu.SemaphoreType.REGULAR((4,)),
                 pltpu.SemaphoreType.DMA((6,)),
                 pltpu.SemaphoreType.DMA((6,)),
                 pltpu.SemaphoreType.DMA((chips,)),
@@ -378,7 +432,7 @@
                 pltpu.SemaphoreType.DMA((chips,)),
                 pltpu.SemaphoreType.DMA((chips,)),
             ],
-            compiler_params=pltpu.CompilerParams(collective_id=0, has_side_effects=True),
+            compiler_params=pltpu.CompilerParams(collective_id=0, has_side_effects=True, vmem_limit_bytes=56 * 10**6),
         )(volume, tf_color, tf_opacity)
 
     return jax.shard_map(

time: 24.5 us -> 22.7 us (0.927)
  Pallas kernels: 22.8 us -> 20.4 us
  local copies, waits for them, and re-layouts: 1.38 us -> 1.95 us
    pallas_call x1, Pallas kernels: 22.8 us -> 20.4 us  [on_device(): pl.pallas_call(lambda *refs: kernel(counts, *refs), name='render', out_sh...]
    unnamed x1 -> x5, local copies, waits for them, and re-layouts: 1.38 us -> 1.95 us
where the time goes in v3:
time: 22.7 us; the launch traced here: 22.3 us
  Pallas kernels  20.4 us (90%)
  local copies, waits for them, and re-layouts  1.95 us (9%)
    pallas_call x1, Pallas kernels, on_device(): pl.pallas_call(lambda *refs: kernel(counts, *refs), name='render', out_sh...  20.4 us
    unnamed x5, local copies, waits for them, and re-layouts  1.95 us

profile of v3, /device:TPU:1, one launch (start us, length us, event | category | flops | bytes accessed | tf_op | source)
XLA Modules:
  0.0 22.3 jit_solution(12729435861889662124)
XLA Ops:
  0.0 0.0 copy-start
  0.0 0.7 %copy-done = f32[3,16]{1,0:T(4,128)S(1)} copy-done((f32[3,16]{1,0:T(4,128)S(1)}, f32[3,16]{1,0:T(4,128)}, u32[]{:S(2)}) %copy-start) | copy-done | bytes 216
  0.7 0.0 copy-start.1
  0.7 0.7 %copy-done.1 = f32[16]{0:T(128)S(1)} copy-done((f32[16]{0:T(128)S(1)}, f32[16]{0:T(128)}, u32[]{:S(2)}) %copy-start.1) | copy-done | bytes 88
  1.3 20.4 %render.1 = f32[4,1,16,128]{3,2,1,0:T(8,128)S(1)} custom-call(bf16[16,256,128]{2,1,0:T(8,128)(2,1)} %refs_0_.1, f32[3,16]{1,0:T(4,128)S(1)} %copy-done, f32[16]{0:T(128)S(1)} %copy-done.1), custom_call_target="tpu_custom_call" | custom-call | tf_op jit(solution)/shard_map/render/pallas_call | solution.py:399
  21.7 0.6 %copy.5 = f32[4,1,16,128]{3,2,1,0:T(8,128)} copy(f32[4,1,16,128]{3,2,1,0:T(8,128)S(1)} %render.1) | data formatting | bytes 65536
Async XLA Ops:
  0.0 0.7 %copy-start = (f32[3,16]{1,0:T(4,128)S(1)}, f32[3,16]{1,0:T(4,128)}, u32[]{:S(2)}) copy-start(f32[3,16]{1,0:T(4,128)} %refs_1_.1) | copy-start | bytes 580
  0.7 0.7 %copy-start.1 = (f32[16]{0:T(128)S(1)}, f32[16]{0:T(128)}, u32[]{:S(2)}) copy-start(f32[16]{0:T(128)} %refs_2_.1) | copy-start | bytes 196

commit v4 on v3

--- a/solution.py
+++ b/solution.py
@@ -20,24 +20,24 @@
 STRIP = 16
 HALF = 8
 CORES = 2
+TRIP = 4
 
 
 def tables_of(color_ref, opacity_ref, knots, scales):
     row = lax.broadcasted_iota(jnp.int32, (HALF, LANES), 0)
-    lane = lax.broadcasted_iota(jnp.int32, (HALF, LANES), 1)
-    pairs = []
+    tables = []
     for channel in range(4):
         at_knot = [
             (color_ref[channel, k] if channel < 3 else opacity_ref[k]) * scales[channel] for k in range(knots)
         ]
-        odd = jnp.zeros((HALF, LANES), jnp.float32)
-        slope = jnp.zeros((HALF, LANES), jnp.float32)
-        for k in range(1, knots, 2):
-            odd = jnp.where(row == k // 2, at_knot[k], odd)
-        for k in range(knots - 1):
-            slope = jnp.where(lane == k, at_knot[k + 1] - at_knot[k], slope)
-        pairs.append((odd, slope))
-    return pairs
+        rise = [at_knot[k + 1] - at_knot[k] for k in range(knots - 1)] + [0.0]
+        odd, below, above = [jnp.zeros((HALF, LANES), jnp.float32) for _ in range(3)]
+        for j in range(knots // 2):
+            odd = jnp.where(row == j, at_knot[2 * j + 1], odd)
+            below = jnp.where(row == j, rise[2 * j], below)
+            above = jnp.where(row == j, rise[2 * j + 1], above)
+        tables.append((odd, below, above))
+    return tables
 
 
 def look_up(table, index, axis):
@@ -63,12 +63,12 @@
     opacity_ref,
     cells,
     wide,
+    looked,
     edges,
     edges_left,
     edges_right,
     across,
-    diff_even,
-    diff_odd,
+    diffs,
     picked,
     parts,
     theirs,
@@ -134,6 +134,22 @@
     first_lane = group_of + (group_of // depth) * depth
     own = (lane_of == first_lane) | (lane_of == first_lane + depth)
     picked[...] = own.astype(jnp.float32).astype(jnp.bfloat16)
+
+    scale = (knots - 1) / (VALUE_HIGH - VALUE_LOW)
+    square = (2.0 * scale) ** 2
+    light = DIFFUSE * LIGHT_Z
+    scales = [light] * 3 + [-2.0 * square * math.log2(math.e) / (depth * views)]
+
+    def placed(some):
+        return some.astype(jnp.float32) * scale - VALUE_LOW * scale
+
+    k = lax.broadcasted_iota(jnp.int32, (2 * LANES, LANES), 0)
+    n = lax.broadcasted_iota(jnp.int32, (2 * LANES, LANES), 1)
+    inside = k < LANES
+    place = k & (2 * depth - 1)
+    plus = (inside & (k == n + 1)) | ((k >= LANES) & (place >= depth) & (n == LANES - 1))
+    minus = (inside & (k == n - 1)) | ((k >= LANES) & (place < depth) & (n == 0))
+    across[...] = ((plus.astype(jnp.float32) - minus.astype(jnp.float32)) * scale).astype(jnp.bfloat16)
 
     pl.semaphore_wait(barrier, expected)
 
@@ -173,6 +189,10 @@
     rounds = max(chips // 2 - 1, 0).bit_length()
     heard = [greet(ready_sem.at[0], 1)] if rounds > 0 else []
 
+    for one in loads:
+        one.wait()
+    tables = tables_of(color_ref, opacity_ref, knots, scales)
+
     load.wait()
 
     narrow = lax.broadcasted_iota(jnp.int32, (STRIP, LANES), 1)
@@ -201,33 +221,23 @@
         def _():
             landings[i][...] = jnp.zeros(landings[i].shape, landings[i].dtype)
 
-    scale = (knots - 1) / (VALUE_HIGH - VALUE_LOW)
-    square = (2.0 * scale) ** 2
-    light = DIFFUSE * LIGHT_Z
-    scales = [light] * 3 + [-2.0 * square * math.log2(math.e) / (depth * views)]
-
-    def placed(some):
-        return some.astype(jnp.float32) * scale - VALUE_LOW * scale
-
-    for one in loads:
-        one.wait()
-    tables = tables_of(color_ref, opacity_ref, knots, scales)
-
-    k = lax.broadcasted_iota(jnp.int32, (2 * LANES, LANES), 0)
-    n = lax.broadcasted_iota(jnp.int32, (2 * LANES, LANES), 1)
-    inside = k < LANES
-    place = k & (2 * depth - 1)
-    plus = (inside & (k == n + 1)) | ((k >= LANES) & (place >= depth) & (n == LANES - 1))
-    minus = (inside & (k == n - 1)) | ((k >= LANES) & (place < depth) & (n == 0))
-    across[...] = ((plus.astype(jnp.float32) - minus.astype(jnp.float32)) * scale).astype(jnp.bfloat16)
-
-    def widen(s, carry):
+    def classify(s, carry):
         for z in range(depth):
-            some = cells[1 + z, pl.ds(pl.multiple_of(STRIP + s * STRIP, STRIP), STRIP)]
-            wide[z, pl.ds(pl.multiple_of(HALF + s * STRIP, HALF), STRIP)] = placed(some)
+            both = placed(cells[1 + z, pl.ds(pl.multiple_of(STRIP + s * STRIP, STRIP), STRIP)])
+            for h in range(2):
+                value = both[h * HALF : (h + 1) * HALF]
+                base = pl.multiple_of(s * STRIP, STRIP) + h * HALF
+                wide[z, pl.ds(base + HALF, HALF)] = value
+                scaled = jnp.clip(value, 0.0, knots - 1.0)
+                interval = scaled.astype(jnp.int32)
+                pair = lax.shift_right_logical(interval, 1)
+                away = scaled - (interval | 1).astype(jnp.float32)
+                for channel, (odd, below, above) in enumerate(tables):
+                    tilt = jnp.where(away < 0.0, look_up(below, pair, 0), look_up(above, pair, 0))
+                    looked[channel, z, pl.ds(base, HALF)] = look_up(odd, pair, 0) + tilt * away
         return carry
 
-    lax.fori_loop(0, height // STRIP, widen, 0)
+    lax.fori_loop(0, height // STRIP, classify, 0)
 
     for i in range(6):
 
@@ -243,9 +253,9 @@
 
     def difference_x(s):
         inner = pl.ds(pl.multiple_of(s * STRIP + STRIP, STRIP), STRIP)
-        b = pl.ds(pl.multiple_of(lax.rem(s * STRIP, group_rows), STRIP), STRIP)
+        b = pl.ds(pl.multiple_of((s * STRIP) & (group_rows - 1), STRIP), STRIP)
         outside = jnp.where(from_left, edges_left[b].astype(jnp.float32), edges_right[b].astype(jnp.float32))
-        mine = picked[pl.ds((s * STRIP // group_rows) * depth, depth)]
+        mine = picked[pl.ds(lax.shift_right_logical(s * STRIP, group_rows.bit_length() - 1) * depth, depth)]
         outside = outside.astype(jnp.bfloat16)[None] * mine
         middle = cells[pl.ds(1, depth), inner]
         left_hand = jnp.concatenate(
@@ -254,6 +264,7 @@
         return jnp.dot(left_hand, across[...], preferred_element_type=jnp.float32)
 
     def partial_image(s, diff):
+        diff[...] = difference_x(s)
         inner = pl.ds(pl.multiple_of(s * STRIP + STRIP, STRIP), STRIP)
         colour = [[jnp.zeros((HALF, LANES), jnp.float32)] * 3 for _ in range(2)]
         through = [jnp.ones((HALF, LANES), jnp.float32) for _ in range(2)]
@@ -264,7 +275,6 @@
                 base = pl.multiple_of(s * STRIP, STRIP) + h * HALF
                 part = slice(h * HALF, (h + 1) * HALF)
                 here = pl.ds(base + HALF, HALF)
-                value = wide[z, here]
                 behind = wide[z - 1, here] if z > 0 else first[part]
                 ahead = wide[z + 1, here] if z + 1 < depth else last[part]
                 gz = ahead - behind
@@ -273,13 +283,7 @@
                 root = lax.rsqrt(gz * gz + gy * gy + (gx * gx + square))
                 lit = jnp.abs(gz + (LIGHT_Y / LIGHT_Z) * gy + (LIGHT_X / LIGHT_Z) * gx)
                 shading = AMBIENT / light + lit * root
-                scaled = jnp.clip(value, 0.0, knots - 1.0)
-                interval = scaled.astype(jnp.int32)
-                pair = lax.shift_right_logical(interval, 1)
-                away = scaled - (interval | 1).astype(jnp.float32)
-                red, green, blue, extinction = [
-                    look_up(odd, pair, 0) + look_up(slope, interval, 1) * away for odd, slope in tables
-                ]
+                red, green, blue, extinction = [looked[channel, z, pl.ds(base, HALF)] for channel in range(4)]
                 passed = jnp.exp2(extinction * (1.2 / square - root * root))
                 after = through[h] * passed
                 weight = (through[h] - after) * shading
@@ -290,9 +294,9 @@
             jnp.concatenate(through, axis=0)
         ]
 
-    def chip_of(i):
-        ahead = jnp.where(i % 2 == 0, chips // 2 - i // 2, chips // 2 + (i + 1) // 2)
-        return lax.rem(chip + ahead, chips)
+    def chip_of(t, k):
+        step = t * (TRIP // 2) + (k + 1) // 2
+        return (chip + chips // 2 + (step if k % 2 else -step)) & (chips - 1)
 
     def swap(i):
         return pltpu.make_async_remote_copy(
@@ -314,51 +318,45 @@
             device_id_type=MESH,
         )
 
-    def strip_of(step):
-        side = jnp.where(step < chips, 1 - core, core)
-        return CORES * chip_of(lax.rem(step, chips)) + side
-
-    diff_even[...] = difference_x(strip_of(0))
-
     def give(t, carry):
-        for odd, diff, following in ((0, diff_even, diff_odd), (1, diff_odd, diff_even)):
-            i = 2 * t + odd
-            following[...] = difference_x(strip_of(i + 1))
-            image = partial_image(strip_of(i), diff)
+        for k in range(TRIP):
+            i = TRIP * t + k
+            image = partial_image(CORES * chip_of(t, k) + 1 - core, diffs.at[k])
             for channel in range(4):
                 parts[i, channel] = image[channel]
-            swap(i).start()
+        for k in range(TRIP):
+            swap(TRIP * t + k).start()
         return carry
 
-    lax.fori_loop(0, chips // 2, give, 0)
+    lax.fori_loop(0, chips // TRIP, give, 0)
 
     def merge(t, carry):
-        for odd in range(2):
-            swap(2 * t + odd).wait_recv()
-        for odd, diff, following in ((0, diff_even, diff_odd), (1, diff_odd, diff_even)):
-            i = 2 * t + odd
-            to_chip = chip_of(i)
-            following[...] = difference_x(strip_of(lax.rem(chips + i + 1, views)))
-            image = partial_image(strip_of(chips + i), diff)
+        for k in range(TRIP):
+            swap(TRIP * t + k).wait_recv()
+        for k in range(TRIP):
+            to_chip = chip_of(t, k)
+            image = partial_image(CORES * to_chip + core, diffs.at[k])
             front, back = [], []
             for channel in range(4):
-                other = theirs[i, channel]
+                other = theirs[TRIP * t + k, channel]
                 front.append(jnp.where(core == 0, image[channel], other))
                 back.append(jnp.where(core == 0, other, image[channel]))
             for channel in range(3):
                 outgoing[to_chip, channel] = (front[channel] + front[3] * back[channel]).astype(jnp.bfloat16)
             outgoing[to_chip, 3] = (1.0 - front[3] * back[3]).astype(jnp.bfloat16)
-            if odd == 0:
+            if k % 2:
+                hand_over(chip_of(t, k - 1), chip).start()
+            if k % 2 and k < TRIP - 1:
                 hand_over(to_chip, chip).start()
-            else:
-
-                @pl.when(to_chip != chip)
-                def _():
-                    hand_over(to_chip, chip).start()
+        to_chip = chip_of(t, TRIP - 1)
+
+        @pl.when(to_chip != chip)
+        def _():
+            hand_over(to_chip, chip).start()
 
         return carry
 
-    lax.fori_loop(0, chips // 2, merge, 0)
+    lax.fori_loop(0, chips // TRIP, merge, 0)
 
     for i in range(6):
 
@@ -411,12 +409,12 @@
                 pltpu.SMEM(tf_opacity.shape, full),
                 pltpu.VMEM((depth + 2, height + 2 * STRIP, width), half),
                 pltpu.VMEM((depth, height + 2 * HALF, width), full),
+                pltpu.VMEM((4, depth, height, width), full),
                 pltpu.VMEM((edge_rows, width), half),
                 pltpu.VMEM((edge_rows, width), half),
                 pltpu.VMEM((edge_rows, width), half),
                 pltpu.VMEM((2 * width, width), half),
-                pltpu.VMEM((depth * STRIP, width), full),
-                pltpu.VMEM((depth * STRIP, width), full),
+                pltpu.VMEM((TRIP, depth * STRIP, width), full),
                 pltpu.VMEM((LANES // 2, STRIP, width), half),
                 pltpu.VMEM((chips, 4, STRIP, width), full),
                 pltpu.VMEM((chips, 4, STRIP, width), full),
@@ -433,7 +431,7 @@
                 pltpu.SemaphoreType.DMA((chips,)),
             ],
             compiler_params=pltpu.CompilerParams(collective_id=0, has_side_effects=True, vmem_limit_bytes=56 * 10**6),
-        )(volume, tf_color, tf_opacity)
+        )(*[pltpu.with_memory_space_constraint(x, pltpu.HBM) for x in (volume, tf_color, tf_opacity)])
 
     return jax.shard_map(
         on_device,

time: 22.7 us -> 21.2 us (0.934); the launches traced: 22.3 us -> 21.1 us
  local copies, waits for them, and re-layouts: 1.95 us -> 0.62 us
    unnamed x5 -> x1, local copies, waits for them, and re-layouts: 1.95 us -> 0.62 us
where the time goes in v4:
time: 21.2 us; the launch traced here: 21.1 us
  Pallas kernels  20.5 us (97%)
  local copies, waits for them, and re-layouts  0.62 us (3%)
    pallas_call x1, Pallas kernels, on_device(): pl.pallas_call(lambda *refs: kernel(counts, *refs), name='render', out_sh...  20.5 us
    unnamed x1, local copies, waits for them, and re-layouts  0.62 us

profile of v4, /device:TPU:1, one launch (start us, length us, event | category | flops | bytes accessed | tf_op | source)
XLA Modules:
  0.0 21.1 jit_solution(6326778093126715814)
XLA Ops:
  0.0 20.5 %render.1 = f32[4,1,16,128]{3,2,1,0:T(8,128)S(1)} custom-call(bf16[16,256,128]{2,1,0:T(8,128)(2,1)} %refs_0_.1, f32[3,16]{1,0:T(4,128)} %refs_1_.1, f32[16]{0:T(128)} %refs_2_.1), custom_call_target="tpu_custom_call" | custom-call | tf_op jit(solution)/shard_map/render/pallas_call | solution.py:397
  20.5 0.6 %copy.5 = f32[4,1,16,128]{3,2,1,0:T(8,128)} copy(f32[4,1,16,128]{3,2,1,0:T(8,128)S(1)} %render.1) | data formatting | bytes 65536

commit v5 on v4

--- a/solution.py
+++ b/solution.py
@@ -30,7 +30,7 @@
         at_knot = [
             (color_ref[channel, k] if channel < 3 else opacity_ref[k]) * scales[channel] for k in range(knots)
         ]
-        rise = [at_knot[k + 1] - at_knot[k] for k in range(knots - 1)] + [0.0]
+        rise = [2.0 * (at_knot[k + 1] - at_knot[k]) for k in range(knots - 1)] + [0.0]
         odd, below, above = [jnp.zeros((HALF, LANES), jnp.float32) for _ in range(3)]
         for j in range(knots // 2):
             odd = jnp.where(row == j, at_knot[2 * j + 1], odd)
@@ -79,6 +79,8 @@
     ready_sem,
     halo_send,
     halo_recv,
+    edge_send,
+    edge_recv,
     swap_send,
     swap_recv,
     part_send,
@@ -88,8 +90,7 @@
     chips = views // CORES
     depth, height, _ = volume.shape
     knots = color_ref.shape[1]
-    groups = LANES // (2 * depth)
-    group_rows = height // groups
+    trips = chips // TRIP
     v, r, c = lax.axis_index("view"), lax.axis_index("row"), lax.axis_index("col")
     core, chip = lax.rem(v, CORES), v // CORES
     partner = v + 1 - 2 * core
@@ -129,19 +130,20 @@
 
     expected = expected + greet(barrier, 1)
 
-    group_of = lax.broadcasted_iota(jnp.int32, (groups * depth, STRIP, LANES), 0)
-    lane_of = lax.broadcasted_iota(jnp.int32, (groups * depth, STRIP, LANES), 2)
+    group_of = lax.broadcasted_iota(jnp.int32, (TRIP * depth, STRIP, LANES), 0)
+    lane_of = lax.broadcasted_iota(jnp.int32, (TRIP * depth, STRIP, LANES), 2)
     first_lane = group_of + (group_of // depth) * depth
     own = (lane_of == first_lane) | (lane_of == first_lane + depth)
     picked[...] = own.astype(jnp.float32).astype(jnp.bfloat16)
 
-    scale = (knots - 1) / (VALUE_HIGH - VALUE_LOW)
+    scale = (knots - 1) / (VALUE_HIGH - VALUE_LOW) / 2
+    shift = -VALUE_LOW * scale - 0.5
     square = (2.0 * scale) ** 2
     light = DIFFUSE * LIGHT_Z
     scales = [light] * 3 + [-2.0 * square * math.log2(math.e) / (depth * views)]
 
     def placed(some):
-        return some.astype(jnp.float32) * scale - VALUE_LOW * scale
+        return some.astype(jnp.float32) * scale + shift
 
     k = lax.broadcasted_iota(jnp.int32, (2 * LANES, LANES), 0)
     n = lax.broadcasted_iota(jnp.int32, (2 * LANES, LANES), 1)
@@ -151,15 +153,11 @@
     minus = (inside & (k == n - 1)) | ((k >= LANES) & (place < depth) & (n == 0))
     across[...] = ((plus.astype(jnp.float32) - minus.astype(jnp.float32)) * scale).astype(jnp.bfloat16)
 
-    pl.semaphore_wait(barrier, expected)
-
     sources = [
         volume.at[pl.ds(0, 1)],
         volume.at[pl.ds(depth - 1, 1)],
         volume.at[:, pl.ds(0, STRIP)],
         volume.at[:, pl.ds(height - STRIP, STRIP)],
-        edges,
-        edges,
     ]
     landings = [
         cells.at[pl.ds(depth + 1, 1), body],
@@ -178,68 +176,91 @@
             device_id=beside[i][1],
             device_id_type=MESH,
         )
-        for i in range(6)
+        for i in range(4)
     ]
-    for i in range(4):
-
-        @pl.when(beside[i][0])
-        def _():
-            copies[i].start()
-
-    rounds = max(chips // 2 - 1, 0).bit_length()
-    heard = [greet(ready_sem.at[0], 1)] if rounds > 0 else []
+
+    def edge_copy(i, q):
+        return pltpu.make_async_remote_copy(
+            src_ref=edges.at[q],
+            dst_ref=landings[i].at[q],
+            send_sem=edge_send.at[i - 4, q],
+            recv_sem=edge_recv.at[i - 4, q],
+            device_id=beside[i][1],
+            device_id_type=MESH,
+        )
+
+    for i in range(6):
+
+        @pl.when(jnp.logical_not(beside[i ^ 1][0]))
+        def _():
+            landings[i][...] = jnp.zeros(landings[i].shape, landings[i].dtype)
+
+    def chip_of(t, k):
+        step = t * (TRIP // 2) + (k + 1) // 2
+        return (chip + chips // 2 + (step if k % 2 else -step)) & (chips - 1)
 
     for one in loads:
         one.wait()
     tables = tables_of(color_ref, opacity_ref, knots, scales)
-
-    load.wait()
-
     narrow = lax.broadcasted_iota(jnp.int32, (STRIP, LANES), 1)
     from_left = (narrow & (2 * depth - 1)) < depth
     taken = jnp.where(from_left, LANES - 1, 0).astype(jnp.int16)
-    for b in range(group_rows // STRIP):
+    rounds = max(chips // 2 - 1, 0).bit_length()
+    ways = [len({2**k, chips - 2**k}) for k in range(rounds)]
+    load.wait()
+
+    def classify(q, carry):
+        side = jnp.where(q < trips, 1 - core, core)
         packed = jnp.zeros((STRIP, LANES), jnp.bfloat16)
-        for g in range(groups):
+        for k in range(TRIP):
+            s = CORES * chip_of(q & (trips - 1), k) + side
             for z in range(depth):
-                row = cells[1 + z, pl.ds(STRIP + g * group_rows + b * STRIP, STRIP)]
-                packed = packed + look_up(row, taken, 1) * picked[g * depth + z]
-        edges[pl.ds(b * STRIP, STRIP)] = packed
-    for i in range(4, 6):
-
-        @pl.when(beside[i][0])
-        def _():
-            copies[i].start()
-
-    for k in range(1, rounds):
-        pl.semaphore_wait(ready_sem.at[k - 1], heard[-1])
-        heard.append(greet(ready_sem.at[k], 2**k))
-
-    for i in range(6):
-
-        @pl.when(jnp.logical_not(beside[i ^ 1][0]))
-        def _():
-            landings[i][...] = jnp.zeros(landings[i].shape, landings[i].dtype)
-
-    def classify(s, carry):
-        for z in range(depth):
-            both = placed(cells[1 + z, pl.ds(pl.multiple_of(STRIP + s * STRIP, STRIP), STRIP)])
-            for h in range(2):
-                value = both[h * HALF : (h + 1) * HALF]
-                base = pl.multiple_of(s * STRIP, STRIP) + h * HALF
-                wide[z, pl.ds(base + HALF, HALF)] = value
-                scaled = jnp.clip(value, 0.0, knots - 1.0)
-                interval = scaled.astype(jnp.int32)
-                pair = lax.shift_right_logical(interval, 1)
-                away = scaled - (interval | 1).astype(jnp.float32)
-                for channel, (odd, below, above) in enumerate(tables):
-                    tilt = jnp.where(away < 0.0, look_up(below, pair, 0), look_up(above, pair, 0))
-                    looked[channel, z, pl.ds(base, HALF)] = look_up(odd, pair, 0) + tilt * away
+                row = cells[1 + z, pl.ds(pl.multiple_of(STRIP + s * STRIP, STRIP), STRIP)]
+                packed = packed + look_up(row, taken, 1) * picked[k * depth + z]
+                both = placed(row)
+                for h in range(2):
+                    value = both[h * HALF : (h + 1) * HALF]
+                    base = pl.multiple_of(s * STRIP, STRIP) + h * HALF
+                    wide[z, pl.ds(base + HALF, HALF)] = value
+                    held = jnp.clip(value, -0.5, knots / 2 - 1.0)
+                    nearest = jnp.round(held)
+                    away = held - nearest
+                    pair = nearest.astype(jnp.int32)
+                    for channel, (odd, below, above) in enumerate(tables):
+                        tilt = jnp.where(away < 0.0, look_up(below, pair, 0), look_up(above, pair, 0))
+                        looked[channel, z, pl.ds(base, HALF)] = look_up(odd, pair, 0) + tilt * away
+        edges[q] = packed
+
+        @pl.when(q == 0)
+        def _():
+            pl.semaphore_wait(barrier, expected)
+            for i in range(4):
+
+                @pl.when(beside[i][0])
+                def _():
+                    copies[i].start()
+
+            if rounds > 0:
+                greet(ready_sem.at[0], 1)
+
+        for k in range(1, rounds):
+
+            @pl.when(q == k)
+            def _():
+                pl.semaphore_wait(ready_sem.at[k - 1], ways[k - 1])
+                greet(ready_sem.at[k], 2**k)
+
+        for i in range(4, 6):
+
+            @pl.when(beside[i][0])
+            def _():
+                edge_copy(i, q).start()
+
         return carry
 
-    lax.fori_loop(0, height // STRIP, classify, 0)
-
-    for i in range(6):
+    lax.fori_loop(0, 2 * trips, classify, 0)
+
+    for i in range(4):
 
         @pl.when(beside[i ^ 1][0])
         def _():
@@ -248,23 +269,28 @@
     for z in range(depth):
         wide[z, pl.ds(0, HALF)] = placed(cells[1 + z, pl.ds(0, STRIP)])[HALF:]
         wide[z, pl.ds(HALF + height, HALF)] = placed(cells[1 + z, pl.ds(STRIP + height, STRIP)])[:HALF]
-    if rounds > 0:
-        pl.semaphore_wait(ready_sem.at[rounds - 1], heard[-1])
-
-    def difference_x(s):
+
+    def edges_of(q):
+        for i in range(4, 6):
+
+            @pl.when(beside[i ^ 1][0])
+            def _():
+                edge_copy(i, q).wait_recv()
+
+        return jnp.where(from_left, edges_left[q].astype(jnp.float32), edges_right[q].astype(jnp.float32))
+
+    def difference_x(s, k, beyond):
         inner = pl.ds(pl.multiple_of(s * STRIP + STRIP, STRIP), STRIP)
-        b = pl.ds(pl.multiple_of((s * STRIP) & (group_rows - 1), STRIP), STRIP)
-        outside = jnp.where(from_left, edges_left[b].astype(jnp.float32), edges_right[b].astype(jnp.float32))
-        mine = picked[pl.ds(lax.shift_right_logical(s * STRIP, group_rows.bit_length() - 1) * depth, depth)]
-        outside = outside.astype(jnp.bfloat16)[None] * mine
+        outside = beyond.astype(jnp.bfloat16)[None] * picked[pl.ds(k * depth, depth)]
         middle = cells[pl.ds(1, depth), inner]
         left_hand = jnp.concatenate(
             [middle.reshape(depth * STRIP, LANES), outside.reshape(depth * STRIP, LANES)], axis=1
         )
         return jnp.dot(left_hand, across[...], preferred_element_type=jnp.float32)
 
-    def partial_image(s, diff):
-        diff[...] = difference_x(s)
+    def partial_image(s, k, beyond):
+        diff = diffs.at[k]
+        diff[...] = difference_x(s, k, beyond)
         inner = pl.ds(pl.multiple_of(s * STRIP + STRIP, STRIP), STRIP)
         colour = [[jnp.zeros((HALF, LANES), jnp.float32)] * 3 for _ in range(2)]
         through = [jnp.ones((HALF, LANES), jnp.float32) for _ in range(2)]
@@ -294,10 +320,6 @@
             jnp.concatenate(through, axis=0)
         ]
 
-    def chip_of(t, k):
-        step = t * (TRIP // 2) + (k + 1) // 2
-        return (chip + chips // 2 + (step if k % 2 else -step)) & (chips - 1)
-
     def swap(i):
         return pltpu.make_async_remote_copy(
             src_ref=parts.at[i],
@@ -319,23 +341,27 @@
         )
 
     def give(t, carry):
+        beyond = edges_of(t)
         for k in range(TRIP):
             i = TRIP * t + k
-            image = partial_image(CORES * chip_of(t, k) + 1 - core, diffs.at[k])
+            image = partial_image(CORES * chip_of(t, k) + 1 - core, k, beyond)
             for channel in range(4):
                 parts[i, channel] = image[channel]
         for k in range(TRIP):
             swap(TRIP * t + k).start()
         return carry
 
-    lax.fori_loop(0, chips // TRIP, give, 0)
+    lax.fori_loop(0, trips, give, 0)
+    if rounds > 0:
+        pl.semaphore_wait(ready_sem.at[rounds - 1], ways[-1])
 
     def merge(t, carry):
+        beyond = edges_of(trips + t)
         for k in range(TRIP):
             swap(TRIP * t + k).wait_recv()
         for k in range(TRIP):
             to_chip = chip_of(t, k)
-            image = partial_image(CORES * to_chip + core, diffs.at[k])
+            image = partial_image(CORES * to_chip + core, k, beyond)
             front, back = [], []
             for channel in range(4):
                 other = theirs[TRIP * t + k, channel]
@@ -344,9 +370,9 @@
             for channel in range(3):
                 outgoing[to_chip, channel] = (front[channel] + front[3] * back[channel]).astype(jnp.bfloat16)
             outgoing[to_chip, 3] = (1.0 - front[3] * back[3]).astype(jnp.bfloat16)
-            if k % 2:
-                hand_over(chip_of(t, k - 1), chip).start()
-            if k % 2 and k < TRIP - 1:
+            if k == 1:
+                hand_over(chip_of(t, 0), chip).start()
+            if 0 < k < TRIP - 1:
                 hand_over(to_chip, chip).start()
         to_chip = chip_of(t, TRIP - 1)
 
@@ -356,13 +382,17 @@
 
         return carry
 
-    lax.fori_loop(0, chips // TRIP, merge, 0)
+    lax.fori_loop(0, trips, merge, 0)
 
     for i in range(6):
 
         @pl.when(beside[i][0])
         def _():
-            copies[i].wait_send()
+            if i < 4:
+                copies[i].wait_send()
+            else:
+                for q in range(2 * trips):
+                    edge_copy(i, q).wait_send()
 
     for i in range(chips):
         swap(i).wait_send()
@@ -393,7 +423,7 @@
         views = counts[0]
         chips = views // CORES
         half, full = jnp.bfloat16, jnp.float32
-        edge_rows = height * 2 * depth // LANES
+        tiles = height // STRIP // TRIP
         return pl.pallas_call(
             lambda *refs: kernel(counts, *refs),
             name="render",
@@ -410,12 +440,12 @@
                 pltpu.VMEM((depth + 2, height + 2 * STRIP, width), half),
                 pltpu.VMEM((depth, height + 2 * HALF, width), full),
                 pltpu.VMEM((4, depth, height, width), full),
-                pltpu.VMEM((edge_rows, width), half),
-                pltpu.VMEM((edge_rows, width), half),
-                pltpu.VMEM((edge_rows, width), half),
+                pltpu.VMEM((tiles, STRIP, width), half),
+                pltpu.VMEM((tiles, STRIP, width), half),
+                pltpu.VMEM((tiles, STRIP, width), half),
                 pltpu.VMEM((2 * width, width), half),
                 pltpu.VMEM((TRIP, depth * STRIP, width), full),
-                pltpu.VMEM((LANES // 2, STRIP, width), half),
+                pltpu.VMEM((TRIP * depth, STRIP, width), half),
                 pltpu.VMEM((chips, 4, STRIP, width), full),
                 pltpu.VMEM((chips, 4, STRIP, width), full),
                 pltpu.VMEM((chips, 4, STRIP, width), half),
@@ -423,8 +453,10 @@
                 pltpu.SemaphoreType.DMA,
                 pltpu.SemaphoreType.DMA((2,)),
                 pltpu.SemaphoreType.REGULAR((4,)),
-                pltpu.SemaphoreType.DMA((6,)),
-                pltpu.SemaphoreType.DMA((6,)),
+                pltpu.SemaphoreType.DMA((4,)),
+                pltpu.SemaphoreType.DMA((4,)),
+                pltpu.SemaphoreType.DMA((2, tiles)),
+                pltpu.SemaphoreType.DMA((2, tiles)),
                 pltpu.SemaphoreType.DMA((chips,)),
                 pltpu.SemaphoreType.DMA((chips,)),
                 pltpu.SemaphoreType.DMA((chips,)),

time: 21.2 us -> 20.9 us (0.986)
  Pallas kernels: 20.5 us -> 20.2 us
    pallas_call x1, Pallas kernels: 20.5 us -> 20.2 us  [on_device(): pl.pallas_call(lambda *refs: kernel(counts, *refs), name='render', out_sh...]
where the time goes in v5:
time: 20.9 us; the launch traced here: 20.8 us
  Pallas kernels  20.2 us (97%)
  local copies, waits for them, and re-layouts  0.62 us (3%)
    pallas_call x1, Pallas kernels, on_device(): pl.pallas_call(lambda *refs: kernel(counts, *refs), name='render', out_sh...  20.2 us
    unnamed x1, local copies, waits for them, and re-layouts  0.62 us

profile of v5, /device:TPU:1, one launch (start us, length us, event | category | flops | bytes accessed | tf_op | source)
XLA Modules:
  0.0 20.8 jit_solution(7387892781407141294)
XLA Ops:
  0.0 20.2 %render.1 = f32[4,1,16,128]{3,2,1,0:T(8,128)S(1)} custom-call(bf16[16,256,128]{2,1,0:T(8,128)(2,1)} %refs_0_.1, f32[3,16]{1,0:T(4,128)} %refs_1_.1, f32[16]{0:T(128)} %refs_2_.1), custom_call_target="tpu_custom_call" | custom-call | tf_op jit(solution)/shard_map/render/pallas_call | solution.py:427
  20.2 0.6 %copy.5 = f32[4,1,16,128]{3,2,1,0:T(8,128)} copy(f32[4,1,16,128]{3,2,1,0:T(8,128)S(1)} %render.1) | data formatting | bytes 65536

commit v6 on v5

--- a/solution.py
+++ b/solution.py
@@ -207,6 +207,15 @@
     taken = jnp.where(from_left, LANES - 1, 0).astype(jnp.int16)
     rounds = max(chips // 2 - 1, 0).bit_length()
     ways = [len({2**k, chips - 2**k}) for k in range(rounds)]
+    pl.semaphore_wait(barrier, expected)
+    for i in range(4):
+
+        @pl.when(beside[i][0])
+        def _():
+            copies[i].start()
+
+    if rounds > 0:
+        greet(ready_sem.at[0], 1)
     load.wait()
 
     def classify(q, carry):
@@ -230,18 +239,6 @@
                         tilt = jnp.where(away < 0.0, look_up(below, pair, 0), look_up(above, pair, 0))
                         looked[channel, z, pl.ds(base, HALF)] = look_up(odd, pair, 0) + tilt * away
         edges[q] = packed
-
-        @pl.when(q == 0)
-        def _():
-            pl.semaphore_wait(barrier, expected)
-            for i in range(4):
-
-                @pl.when(beside[i][0])
-                def _():
-                    copies[i].start()
-
-            if rounds > 0:
-                greet(ready_sem.at[0], 1)
 
         for k in range(1, rounds):
 

time: 20.9 us -> 20.6 us (0.986)
  Pallas kernels: 20.2 us -> 19.8 us
    pallas_call x1, Pallas kernels: 20.2 us -> 19.8 us  [on_device(): pl.pallas_call(lambda *refs: kernel(counts, *refs), name='render', out_sh...]
where the time goes in v6:
time: 20.6 us; the launch traced here: 20.4 us
  Pallas kernels  19.8 us (96%)
  local copies, waits for them, and re-layouts  0.62 us (3%)
    pallas_call x1, Pallas kernels, on_device(): pl.pallas_call(lambda *refs: kernel(counts, *refs), name='render', out_sh...  19.8 us
    unnamed x1, local copies, waits for them, and re-layouts  0.62 us

profile of v6, /device:TPU:1, one launch (start us, length us, event | category | flops | bytes accessed | tf_op | source)
XLA Modules:
  0.0 20.4 jit_solution(8048208805695794131)
XLA Ops:
  0.0 19.8 %render.1 = f32[4,1,16,128]{3,2,1,0:T(8,128)S(1)} custom-call(bf16[16,256,128]{2,1,0:T(8,128)(2,1)} %refs_0_.1, f32[3,16]{1,0:T(4,128)} %refs_1_.1, f32[16]{0:T(128)} %refs_2_.1), custom_call_target="tpu_custom_call" | custom-call | tf_op jit(solution)/shard_map/render/pallas_call | solution.py:424
  19.8 0.6 %copy.5 = f32[4,1,16,128]{3,2,1,0:T(8,128)} copy(f32[4,1,16,128]{3,2,1,0:T(8,128)S(1)} %render.1) | data formatting | bytes 65536
